TPU v7x, 512 devices: a whole 4x4x16 slice. The times are simulated.
512 devices in a mesh: dp: 8 (over z_hi, core), cuts: 16 (over y, x), topic: 4 (over z_lo).
Axes of the slice: x: 4, y: 4, z: 16 (z_hi: 4, z_lo: 4; z = z_hi * 4 + z_lo), core: 2. Of those that a mesh axis runs over, the one named last changes fastest.
Arguments:
- doc_mix: float32 [32768, 4096], P(('dp', 'cuts'), 'topic'), may hold values from 0.01 to 1
- doc_lengths: int32 [32768], P(('dp', 'cuts')), may hold values from 1 to 4096, 8388608 in all
- counts: int32 [32768, 1024], P(('dp', 'cuts')), may hold values from 0 to 7
- tile_on: int32 [128, 16], P(('dp', 'cuts')), may hold values from 0 to 1, as said below
- word_counts: float32 [1024, 4096], P('cuts', 'topic'), may hold values from 0.01 to 10
- topic_totals: float32 [4096], P('topic'), may hold values from 1000 to 100000
Outputs:
- doc_topic: float32 [32768, 4096], P(('dp', 'cuts'), 'topic')
- word_topic: float32 [1024, 4096], P('cuts', 'topic')
Inputs may be any that keep to these rules, and one draw needn't show every extreme that they name: `tile_on`: each block of documents meets at least one word slice.
All inputs are finite; a program needn't handle non-finite values. No bound on the sum of `doc_lengths` on one device may be relied on, other than what follows from the above.
Results may differ from a plain program's by a relative error of at most 0.000078.
Values sent between devices are 32-bit elements; how exact they have to be, the bound alone decides.
No kernel may reach another device: no remote copies, remote signals or barrier semaphores. Data moves between devices by JAX's collectives and lax.ppermute only.
A program may use at most 64 MiB of HBM per device.

v0:
```python
import jax
import jax.numpy as jnp
from jax import lax
from jax.sharding import Mesh, PartitionSpec as P


VOCAB = 1048576
ALPHA = 0.1
BETA = 0.01

CORES = 2
EXTRA = 8


def wrapped(place, size):
    return place & (size - 1)


def moved(block, axis, distance):
    size = lax.axis_size(axis)
    return lax.ppermute(block, axis, [(i, (i + distance) % size) for i in range(size)])


def exchanged(blocks, axes):
    return lax.all_to_all(blocks, axes, 0, 0, tiled=True)


def scattered(sums, axes):
    members = lax.axis_size(axes)
    rows = sums.shape[0] // members
    return jnp.sum(exchanged(sums, axes).reshape(members, rows, sums.shape[1]), axis=0)


def matmul(left, right, contract):
    return lax.dot_general(left, right, (contract, ((), ())), precision=lax.Precision.HIGH, preferred_element_type=jnp.float32)


def shards(doc_mix, doc_lengths, counts, tile_on, word_counts, topic_totals):
    docs, topics = doc_mix.shape
    slice_words = word_counts.shape[0]
    n_zh, n_t = lax.axis_size("zh"), lax.axis_size("t")
    cut = ("y", "x")
    n_cuts = lax.axis_size(cut)
    core, t = lax.axis_index("core"), lax.axis_index("t")
    half = slice_words // CORES
    rows = half // n_zh
    chunk = n_cuts * half // n_t

    scale = (topic_totals + VOCAB * BETA)[None, :]
    own_counts = lax.dynamic_index_in_dim(word_counts.reshape(n_zh, CORES, rows, topics), core, 1, False).reshape(half, topics)
    own_half = (own_counts + BETA) / scale
    copies = jnp.broadcast_to(own_half[None], (n_cuts, half, topics)).reshape(n_cuts * half, topics)
    words = [exchanged(copies, cut)]
    words.append(moved(words[0], "core", 1))

    tiles = jnp.repeat(tile_on[0], slice_words)[:, None]
    weights = (counts.T * tiles).astype(jnp.float32).reshape(n_cuts, n_zh, CORES, rows, docs)

    def chunk_weights(wave):
        start = (t * (n_cuts // n_t), 0, wrapped(core + wave, CORES), 0, 0)
        return lax.dynamic_slice(weights, start, (n_cuts // n_t, n_zh, 1, rows, docs)).reshape(chunk, docs)

    def parts_by_topic(wave, mix, extra):
        products = matmul(words[wave], mix, ((1,), (1,))).reshape(n_t, chunk, docs)
        word_sums = jnp.sum(words[wave], axis=1).reshape(n_t, 1, chunk)
        word_sums = jnp.pad(word_sums, ((0, 0), (0, EXTRA - 1 - len(extra)), (0, docs - chunk)))
        rows_below = [jnp.broadcast_to(row[None, None], (n_t, 1, docs)) for row in extra]
        return jnp.concatenate([products] + rows_below + [word_sums], axis=1)

    def sent_over_topics(blocks):
        return [moved(block, "t", d) for d, block in zip(range(1, n_t), blocks)]

    def by_owner(parts):
        return [lax.dynamic_index_in_dim(parts, wrapped(t + d, n_t), 0, False) for d in range(n_t)]

    def after(arrived, earlier):
        return lax.optimization_barrier((arrived, earlier))[0]

    def assembled(own, arrived):
        ratio = lax.dynamic_update_index_in_dim(jnp.zeros((n_t, chunk, docs), jnp.float32), own, t, 0)
        for d, block in zip(range(1, n_t), arrived):
            ratio = lax.dynamic_update_index_in_dim(ratio, block, wrapped(t - d, n_t), 0)
        return ratio.reshape(n_t * chunk, docs)

    by_doc = ((1,), (0,))
    parts_0 = parts_by_topic(0, doc_mix, [jnp.sum(doc_mix, axis=1)])
    own_0, *given_0 = by_owner(parts_0)
    arrived_0 = sent_over_topics(given_0)
    own_1, *given_1 = by_owner(parts_by_topic(1, after(doc_mix, parts_0), []))
    arrived_1 = sent_over_topics(given_1)

    total = own_0 + sum(after(arrived_0, given_1))
    doc_scale = doc_lengths.astype(jnp.float32) / total[chunk]
    doc_weight = doc_mix * doc_scale[:, None] + ALPHA
    chunk_0 = chunk_weights(0) / (total[:chunk] * doc_scale[None, :] + ALPHA * total[chunk + 1, :chunk][:, None])
    shared_0 = sent_over_topics([chunk_0] * (n_t - 1))

    total = own_1 + sum(after(arrived_1, chunk_0))
    chunk_1 = chunk_weights(1) / (total[:chunk] * doc_scale[None, :] + ALPHA * total[chunk, :chunk][:, None])
    shared_1 = sent_over_topics([chunk_1] * (n_t - 1))

    ratio_0 = assembled(chunk_0, after(shared_0, chunk_1))
    sums_0 = matmul(ratio_0, doc_weight, by_doc)
    ratio_1 = assembled(chunk_1, after(shared_1, sums_0))
    ratios = [ratio_0, ratio_1]

    sums_given = moved(sums_0, "core", 1)
    sums = scattered(matmul(ratios[1], doc_weight, by_doc) + sums_given, cut)
    sums = scattered(sums, "zh")
    word_total = lax.all_gather(sums, ("zh", "core"), tiled=True)
    word_total = word_total.reshape(n_zh, CORES, rows, topics)[:, ::-1].reshape(slice_words, topics)

    by_word = ((0,), (0,))
    doc_sums = matmul(ratios[0], words[0], by_word) + matmul(ratios[1], words[1], by_word)
    return (doc_weight * doc_sums, (word_counts + BETA) / scale * word_total)


def solution(mesh):
    dp, cuts, topic = (mesh.shape[a] for a in ("dp", "cuts", "topic"))
    side = int(round(cuts**0.5))
    finer = Mesh(mesh.devices.reshape(dp // CORES, CORES, cuts // side, side, topic), ("zh", "core", "y", "x", "t"))
    docs, cut = ("zh", "core", "y", "x"), ("y", "x")

    return jax.shard_map(
        shards,
        mesh=finer,
        in_specs=(P(docs, "t"), P(docs), P(docs, None), P(docs, None), P(cut, "t"), P("t")),
        out_specs=(P(docs, "t"), P(cut, "t")),
        check_vma=False,
    )
```

profile of v0, /device:TPU:1, one launch (start us, length us, event | category | flops | bytes accessed | tf_op | source)
XLA Modules:
  0.0 198.9 jit_solution(8495737630587725446)
XLA Ops:
  2.5 34.4 %all_to_all.27 = f32[16,32,1024]{2,1,0:T(8,128)S(1)} all-to-all(f32[16,32,1024]{2,1,0:T(8,128)S(1)} %broadcast_in_dim.44), channel_id=1, replica_groups=mesh['zh'=4,'core'=2,'y'=4,'x'=4,'t'=4] {'y','x'}, dimensions={0} | all-to-all | bytes 4194304 | tf_op jit(solution)/shard_map/all_to_all | solution.py:25
  36.9 4.8 %collective-permute-start.3 = (f32[512,1024]{1,0:T(8,128)S(1)}, f32[512,1024]{1,0:T(8,128)}, u32[]{:S(2)}, u32[]{:S(2)}) collective-permute-start(f32[512,1024]{1,0:T(8,128)S(1)} %bitcast.71), channel_id=1, source_target_pairs={{0,64},{64,0},{1,65},{65,1},{2,66},{66,2},{3,67},{67,3},{4,68},{68... | collective-permute-start | bytes 6291464 | tf_op jit(solution)/shard_map/ppermute | solution.py:21
  41.8 2.5 %copy.11 = s32[256,1024]{0,1:T(8,128)} copy(s32[256,1024]{1,0:T(8,128)} %param.8) | data formatting | bytes 2097152 | tf_op args[2]
  44.6 1.4 multiply_convert_fusion
  49.0 3.0 %collective-permute-start = (f32[136,256]{1,0:T(8,128)}, f32[136,256]{1,0:T(8,128)S(1)}, u32[]{:S(2)}, u32[]{:S(2)}) collective-permute-start(f32[136,256]{1,0:T(8,128)} %get-tuple-element.35), channel_id=1, source_target_pairs={{0,1},{1,2},{2,3},{3,0},{4,5},{5,6},{6,7},{7,4},{8,9},{9,10},{10,1... | collective-permute-start | bytes 417800 | tf_op jit(solution)/shard_map/ppermute | solution.py:21
  52.0 4.9 %collective-permute-start.1 = (f32[136,256]{1,0:T(8,128)}, f32[136,256]{1,0:T(8,128)}, u32[]{:S(2)}, u32[]{:S(2)}) collective-permute-start(f32[136,256]{1,0:T(8,128)} %get-tuple-element.34), channel_id=1, source_target_pairs={{0,2},{1,3},{2,0},{3,1},{4,6},{5,7},{6,4},{7,5},{8,10},{9,11},{10,... | collective-permute-start | bytes 417800 | tf_op jit(solution)/shard_map/ppermute | solution.py:21
  56.9 2.6 %collective-permute-start.2 = (f32[136,256]{1,0:T(8,128)}, f32[136,256]{1,0:T(8,128)}, u32[]{:S(2)}, u32[]{:S(2)}) collective-permute-start(f32[136,256]{1,0:T(8,128)} %get-tuple-element.33), channel_id=1, source_target_pairs={{0,3},{1,0},{2,1},{3,2},{4,7},{5,4},{6,5},{7,6},{8,11},{9,8},{10,9... | collective-permute-start | bytes 417800 | tf_op jit(solution)/shard_map/ppermute | solution.py:21
  59.6 1.8 reduce_sum.47
  61.4 2.6 %fusion.16 = f32[512,256]{1,0:T(8,128)S(1)} fusion(f32[512,1024]{1,0:T(8,128)} %collective-permute-done.3, f32[256,1024]{1,0:T(8,128)S(1)} %copy-done), kind=kOutput, calls=%fused_computation.50 | convolution fusion | flops 805306368 | bytes 3670016 | tf_op jit(solution)/shard_map/dot_general | solution.py:35
  65.2 1.9 collective-permute-done.2
  68.2 3.3 %collective-permute-start.7 = (f32[136,256]{1,0:T(8,128)S(1)}, f32[136,256]{1,0:T(8,128)S(1)}, u32[]{:S(2)}, u32[]{:S(2)}) collective-permute-start(f32[136,256]{1,0:T(8,128)S(1)} %get-tuple-element.32), channel_id=1, source_target_pairs={{0,1},{1,2},{2,3},{3,0},{4,5},{5,6},{6,7},{7,4},{8,9},{9,10},{10,1... | collective-permute-start | bytes 417800 | tf_op jit(solution)/shard_map/ppermute | solution.py:21
  71.5 2.8 %collective-permute-start.8 = (f32[136,256]{1,0:T(8,128)S(1)}, f32[136,256]{1,0:T(8,128)S(1)}, u32[]{:S(2)}, u32[]{:S(2)}) collective-permute-start(f32[136,256]{1,0:T(8,128)S(1)} %get-tuple-element.31), channel_id=1, source_target_pairs={{0,2},{1,3},{2,0},{3,1},{4,6},{5,7},{6,4},{7,5},{8,10},{9,11},{10,... | collective-permute-start | bytes 417800 | tf_op jit(solution)/shard_map/ppermute | solution.py:21
  74.3 3.1 %collective-permute-start.9 = (f32[136,256]{1,0:T(8,128)S(1)}, f32[136,256]{1,0:T(8,128)S(1)}, u32[]{:S(2)}, u32[]{:S(2)}) collective-permute-start(f32[136,256]{1,0:T(8,128)S(1)} %get-tuple-element.30), channel_id=1, source_target_pairs={{0,3},{1,0},{2,1},{3,2},{4,7},{5,4},{6,5},{7,6},{8,11},{9,8},{10,9... | collective-permute-start | bytes 417800 | tf_op jit(solution)/shard_map/ppermute | solution.py:21
  77.6 2.2 %collective-permute-start.4 = (f32[128,256]{1,0:T(8,128)S(1)}, f32[128,256]{1,0:T(8,128)S(1)}, u32[]{:S(2)}, u32[]{:S(2)}) collective-permute-start(f32[128,256]{1,0:T(8,128)S(1)} %get-tuple-element.37), channel_id=1, source_target_pairs={{0,1},{1,2},{2,3},{3,0},{4,5},{5,6},{6,7},{7,4},{8,9},{9,10},{10,1... | collective-permute-start | bytes 393224 | tf_op jit(solution)/shard_map/ppermute | solution.py:21
  79.8 3.4 %collective-permute-start.5 = (f32[128,256]{1,0:T(8,128)S(1)}, f32[128,256]{1,0:T(8,128)S(1)}, u32[]{:S(2)}, u32[]{:S(2)}) collective-permute-start(f32[128,256]{1,0:T(8,128)S(1)} %get-tuple-element.37), channel_id=1, source_target_pairs={{0,2},{1,3},{2,0},{3,1},{4,6},{5,7},{6,4},{7,5},{8,10},{9,11},{10,... | collective-permute-start | bytes 393224 | tf_op jit(solution)/shard_map/ppermute | solution.py:21
  83.2 3.8 %collective-permute-start.6 = (f32[128,256]{1,0:T(8,128)S(1)}, f32[128,256]{1,0:T(8,128)S(1)}, u32[]{:S(2)}, u32[]{:S(2)}) collective-permute-start(f32[128,256]{1,0:T(8,128)S(1)} %get-tuple-element.37), channel_id=1, source_target_pairs={{0,3},{1,0},{2,1},{3,2},{4,7},{5,4},{6,5},{7,6},{8,11},{9,8},{10,9... | collective-permute-start | bytes 393224 | tf_op jit(solution)/shard_map/ppermute | solution.py:21
  87.3 7.7 %collective-permute-done.5 = f32[128,256]{1,0:T(8,128)S(1)} collective-permute-done((f32[128,256]{1,0:T(8,128)S(1)}, f32[128,256]{1,0:T(8,128)S(1)}, u32[]{:S(2)}, u32[]{:S(2)}) %collective-permute-start.5) | collective-permute-done | bytes 131104 | tf_op jit(solution)/shard_map/ppermute | solution.py:21
  95.0 1.2 fusion.3
  96.2 2.5 %collective-permute-start.13 = (f32[512,1024]{1,0:T(8,128)S(1)}, f32[512,1024]{1,0:T(8,128)S(1)}, u32[]{:S(2)}, u32[]{:S(2)}) collective-permute-start(f32[512,1024]{1,0:T(8,128)S(1)} %fusion.3), channel_id=1, source_target_pairs={{0,64},{64,0},{1,65},{65,1},{2,66},{66,2},{3,67},{67,3},{4,68},{68... | collective-permute-start | bytes 6291464 | tf_op jit(solution)/shard_map/ppermute | solution.py:21
  98.7 4.9 %collective-permute-start.10 = (f32[128,256]{1,0:T(8,128)S(1)}, f32[128,256]{1,0:T(8,128)S(1)}, u32[]{:S(2)}, u32[]{:S(2)}) collective-permute-start(f32[128,256]{1,0:T(8,128)S(1)} %get-tuple-element.39), channel_id=1, source_target_pairs={{0,1},{1,2},{2,3},{3,0},{4,5},{5,6},{6,7},{7,4},{8,9},{9,10},{10,1... | collective-permute-start | bytes 393224 | tf_op jit(solution)/shard_map/ppermute | solution.py:21
  103.6 3.1 %collective-permute-start.11 = (f32[128,256]{1,0:T(8,128)S(1)}, f32[128,256]{1,0:T(8,128)S(1)}, u32[]{:S(2)}, u32[]{:S(2)}) collective-permute-start(f32[128,256]{1,0:T(8,128)S(1)} %get-tuple-element.39), channel_id=1, source_target_pairs={{0,2},{1,3},{2,0},{3,1},{4,6},{5,7},{6,4},{7,5},{8,10},{9,11},{10,... | collective-permute-start | bytes 393224 | tf_op jit(solution)/shard_map/ppermute | solution.py:21
  106.8 2.8 %collective-permute-start.12 = (f32[128,256]{1,0:T(8,128)S(1)}, f32[128,256]{1,0:T(8,128)S(1)}, u32[]{:S(2)}, u32[]{:S(2)}) collective-permute-start(f32[128,256]{1,0:T(8,128)S(1)} %get-tuple-element.39), channel_id=1, source_target_pairs={{0,3},{1,0},{2,1},{3,2},{4,7},{5,4},{6,5},{7,6},{8,11},{9,8},{10,9... | collective-permute-start | bytes 393224 | tf_op jit(solution)/shard_map/ppermute | solution.py:21
  109.6 4.9 %collective-permute-done.11 = f32[128,256]{1,0:T(8,128)S(1)} collective-permute-done((f32[128,256]{1,0:T(8,128)S(1)}, f32[128,256]{1,0:T(8,128)S(1)}, u32[]{:S(2)}, u32[]{:S(2)}) %collective-permute-start.11) | collective-permute-done | bytes 131104 | tf_op jit(solution)/shard_map/ppermute | solution.py:21
  114.4 2.0 collective-permute-done.12
  116.5 1.2 convolution_add_fusion
  117.7 30.7 %all_to_all.28 = f32[16,32,1024]{2,1,0:T(8,128)} all-to-all(f32[16,32,1024]{2,1,0:T(8,128)S(1)} %bitcast.74), channel_id=1, replica_groups=mesh['zh'=4,'core'=2,'y'=4,'x'=4,'t'=4] {'y','x'}, dimensions={0} | all-to-all | bytes 4194304 | tf_op jit(solution)/shard_map/all_to_all | solution.py:25
  148.4 2.4 %reduce_sum.48 = f32[32,1024]{1,0:T(8,128)} reduce(f32[16,32,1024]{2,1,0:T(8,128)} %all_to_all.28, f32[]{:T(128)} %constant.70.clone.1), dimensions={0}, to_apply=%region_3.4 | reduce | flops 491520 | bytes 2228228 | tf_op jit(solution)/shard_map/reduce_sum | solution.py:31
  150.8 12.5 %all-to-all-start.2 = ((f32[4,8,1024]{2,1,0:T(8,128)}), f32[4,8,1024]{2,1,0:T(8,128)S(1)}, u32[]{:S(2)}, u32[]{:S(2)}) async-start(f32[4,8,1024]{2,1,0:T(8,128)} %bitcast.35), calls=%async_computation.2 | async-start | bytes 262144 | tf_op jit(solution)/shard_map/all_to_all | solution.py:25
  163.2 2.2 %fusion.17 = f32[256,1024]{1,0:T(8,128)S(1)} fusion(f32[512,256]{1,0:T(8,128)} %bitcast.78, f32[512,1024]{1,0:T(8,128)S(1)} %bitcast.73), kind=kOutput, calls=%fused_computation.51 | convolution fusion | flops 805306368 | bytes 3670016 | tf_op jit(solution)/shard_map/dot_general | solution.py:35
  165.4 3.8 %fusion = f32[256,1024]{1,0:T(8,128)} fusion(f32[256,1024]{1,0:T(8,128)S(1)} %fusion.17, f32[512,256]{1,0:T(8,128)S(1)} %bitcast.76, f32[512,1024]{1,0:T(8,128)} %collective-permute-done.3, f32[256,1024]{1,0:T(8,128)S(1)} %copy-done, f32[256]{0:T(256)S(1)} %convert_divide_fusion), kind=kOutput, calls=%fused_computation.2 | convolution fusion | flops 806354944 | bytes 5768192 | tf_op jit(solution)/shard_map/dot_general | solution.py:35
  169.2 7.5 %all-to-all-done.2 = f32[4,8,1024]{2,1,0:T(8,128)S(1)} async-done(((f32[4,8,1024]{2,1,0:T(8,128)}), f32[4,8,1024]{2,1,0:T(8,128)S(1)}, u32[]{:S(2)}, u32[]{:S(2)}) %all-to-all-start.2) | async-done | bytes 131104 | tf_op jit(solution)/shard_map/all_to_all | solution.py:25
  176.7 21.4 %all_gather.3 = f32[64,1024]{1,0:T(8,128)S(1)} all-gather(f32[8,1024]{1,0:T(8,128)S(1)} %reduce_sum.49), channel_id=1, replica_groups=mesh['zh'=4,'core'=2,'y'=4,'x'=4,'t'=4] {'zh','core'}, dimensions={0}, use_global_device_ids=true | all-gather | bytes 294912 | tf_op jit(solution)/shard_map/all_gather | solution.py:110
  (60 shorter events, 8.6 us)
Async XLA Ops:
  36.9 7.4 %copy-start.7 = (s32[1,16]{1,0:T(1,128)S(1)}, s32[1,16]{1,0:T(1,128)}, u32[]{:S(2)}) copy-start(s32[1,16]{1,0:T(1,128)} %param.9) | copy-start | bytes 196
  36.9 7.5 %copy-start = (f32[256,1024]{1,0:T(8,128)S(1)}, f32[256,1024]{1,0:T(8,128)}, u32[]{:S(2)}) copy-start(f32[256,1024]{1,0:T(8,128)} %param.6) | copy-start | bytes 3145732
  36.9 22.7 %collective-permute-start.3 = (f32[512,1024]{1,0:T(8,128)S(1)}, f32[512,1024]{1,0:T(8,128)}, u32[]{:S(2)}, u32[]{:S(2)}) collective-permute-start(f32[512,1024]{1,0:T(8,128)S(1)} %bitcast.71), channel_id=1, source_target_pairs={{0,64},{64,0},{1,65},{65,1},{2,66},{66,2},{3,67},{67,3},{4,68},{68... | collective-permute-start | bytes 6291464 | tf_op jit(solution)/shard_map/ppermute | solution.py:21
  47.4 0.8 copy-start.4
  49.0 15.1 %collective-permute-start = (f32[136,256]{1,0:T(8,128)}, f32[136,256]{1,0:T(8,128)S(1)}, u32[]{:S(2)}, u32[]{:S(2)}) collective-permute-start(f32[136,256]{1,0:T(8,128)} %get-tuple-element.35), channel_id=1, source_target_pairs={{0,1},{1,2},{2,3},{3,0},{4,5},{5,6},{6,7},{7,4},{8,9},{9,10},{10,1... | collective-permute-start | bytes 417800 | tf_op jit(solution)/shard_map/ppermute | solution.py:21
  52.0 13.2 %collective-permute-start.1 = (f32[136,256]{1,0:T(8,128)}, f32[136,256]{1,0:T(8,128)}, u32[]{:S(2)}, u32[]{:S(2)}) collective-permute-start(f32[136,256]{1,0:T(8,128)} %get-tuple-element.34), channel_id=1, source_target_pairs={{0,2},{1,3},{2,0},{3,1},{4,6},{5,7},{6,4},{7,5},{8,10},{9,11},{10,... | collective-permute-start | bytes 417800 | tf_op jit(solution)/shard_map/ppermute | solution.py:21
  56.9 10.2 %collective-permute-start.2 = (f32[136,256]{1,0:T(8,128)}, f32[136,256]{1,0:T(8,128)}, u32[]{:S(2)}, u32[]{:S(2)}) collective-permute-start(f32[136,256]{1,0:T(8,128)} %get-tuple-element.33), channel_id=1, source_target_pairs={{0,3},{1,0},{2,1},{3,2},{4,7},{5,4},{6,5},{7,6},{8,11},{9,8},{10,9... | collective-permute-start | bytes 417800 | tf_op jit(solution)/shard_map/ppermute | solution.py:21
  64.0 13.5 %copy-start.6 = (s32[256]{0:T(256)S(1)}, s32[256]{0:T(256)}, u32[]{:S(2)}) copy-start(s32[256]{0:T(256)} %param.7) | copy-start | bytes 3076
  68.2 15.0 %collective-permute-start.7 = (f32[136,256]{1,0:T(8,128)S(1)}, f32[136,256]{1,0:T(8,128)S(1)}, u32[]{:S(2)}, u32[]{:S(2)}) collective-permute-start(f32[136,256]{1,0:T(8,128)S(1)} %get-tuple-element.32), channel_id=1, source_target_pairs={{0,1},{1,2},{2,3},{3,0},{4,5},{5,6},{6,7},{7,4},{8,9},{9,10},{10,1... | collective-permute-start | bytes 417800 | tf_op jit(solution)/shard_map/ppermute | solution.py:21
  71.5 15.5 %collective-permute-start.8 = (f32[136,256]{1,0:T(8,128)S(1)}, f32[136,256]{1,0:T(8,128)S(1)}, u32[]{:S(2)}, u32[]{:S(2)}) collective-permute-start(f32[136,256]{1,0:T(8,128)S(1)} %get-tuple-element.31), channel_id=1, source_target_pairs={{0,2},{1,3},{2,0},{3,1},{4,6},{5,7},{6,4},{7,5},{8,10},{9,11},{10,... | collective-permute-start | bytes 417800 | tf_op jit(solution)/shard_map/ppermute | solution.py:21
  74.3 12.7 %collective-permute-start.9 = (f32[136,256]{1,0:T(8,128)S(1)}, f32[136,256]{1,0:T(8,128)S(1)}, u32[]{:S(2)}, u32[]{:S(2)}) collective-permute-start(f32[136,256]{1,0:T(8,128)S(1)} %get-tuple-element.30), channel_id=1, source_target_pairs={{0,3},{1,0},{2,1},{3,2},{4,7},{5,4},{6,5},{7,6},{8,11},{9,8},{10,9... | collective-permute-start | bytes 417800 | tf_op jit(solution)/shard_map/ppermute | solution.py:21
  77.6 9.6 %collective-permute-start.4 = (f32[128,256]{1,0:T(8,128)S(1)}, f32[128,256]{1,0:T(8,128)S(1)}, u32[]{:S(2)}, u32[]{:S(2)}) collective-permute-start(f32[128,256]{1,0:T(8,128)S(1)} %get-tuple-element.37), channel_id=1, source_target_pairs={{0,1},{1,2},{2,3},{3,0},{4,5},{5,6},{6,7},{7,4},{8,9},{9,10},{10,1... | collective-permute-start | bytes 393224 | tf_op jit(solution)/shard_map/ppermute | solution.py:21
  79.8 15.2 %collective-permute-start.5 = (f32[128,256]{1,0:T(8,128)S(1)}, f32[128,256]{1,0:T(8,128)S(1)}, u32[]{:S(2)}, u32[]{:S(2)}) collective-permute-start(f32[128,256]{1,0:T(8,128)S(1)} %get-tuple-element.37), channel_id=1, source_target_pairs={{0,2},{1,3},{2,0},{3,1},{4,6},{5,7},{6,4},{7,5},{8,10},{9,11},{10,... | collective-permute-start | bytes 393224 | tf_op jit(solution)/shard_map/ppermute | solution.py:21
  83.2 11.8 %collective-permute-start.6 = (f32[128,256]{1,0:T(8,128)S(1)}, f32[128,256]{1,0:T(8,128)S(1)}, u32[]{:S(2)}, u32[]{:S(2)}) collective-permute-start(f32[128,256]{1,0:T(8,128)S(1)} %get-tuple-element.37), channel_id=1, source_target_pairs={{0,3},{1,0},{2,1},{3,2},{4,7},{5,4},{6,5},{7,6},{8,11},{9,8},{10,9... | collective-permute-start | bytes 393224 | tf_op jit(solution)/shard_map/ppermute | solution.py:21
  95.0 21.4 %copy-start.3 = (f32[4,128,256]{2,1,0:T(8,128)}, f32[4,128,256]{2,1,0:T(8,128)S(1)}, u32[]{:S(2)}) copy-start(f32[4,128,256]{2,1,0:T(8,128)S(1)} %bitcast_dynamic-update-slice_fusion.4) | copy-start | bytes 1572868
  96.2 20.3 %collective-permute-start.13 = (f32[512,1024]{1,0:T(8,128)S(1)}, f32[512,1024]{1,0:T(8,128)S(1)}, u32[]{:S(2)}, u32[]{:S(2)}) collective-permute-start(f32[512,1024]{1,0:T(8,128)S(1)} %fusion.3), channel_id=1, source_target_pairs={{0,64},{64,0},{1,65},{65,1},{2,66},{66,2},{3,67},{67,3},{4,68},{68... | collective-permute-start | bytes 6291464 | tf_op jit(solution)/shard_map/ppermute | solution.py:21
  98.7 10.8 %collective-permute-start.10 = (f32[128,256]{1,0:T(8,128)S(1)}, f32[128,256]{1,0:T(8,128)S(1)}, u32[]{:S(2)}, u32[]{:S(2)}) collective-permute-start(f32[128,256]{1,0:T(8,128)S(1)} %get-tuple-element.39), channel_id=1, source_target_pairs={{0,1},{1,2},{2,3},{3,0},{4,5},{5,6},{6,7},{7,4},{8,9},{9,10},{10,1... | collective-permute-start | bytes 393224 | tf_op jit(solution)/shard_map/ppermute | solution.py:21
  103.6 10.8 %collective-permute-start.11 = (f32[128,256]{1,0:T(8,128)S(1)}, f32[128,256]{1,0:T(8,128)S(1)}, u32[]{:S(2)}, u32[]{:S(2)}) collective-permute-start(f32[128,256]{1,0:T(8,128)S(1)} %get-tuple-element.39), channel_id=1, source_target_pairs={{0,2},{1,3},{2,0},{3,1},{4,6},{5,7},{6,4},{7,5},{8,10},{9,11},{10,... | collective-permute-start | bytes 393224 | tf_op jit(solution)/shard_map/ppermute | solution.py:21
  106.8 9.6 %collective-permute-start.12 = (f32[128,256]{1,0:T(8,128)S(1)}, f32[128,256]{1,0:T(8,128)S(1)}, u32[]{:S(2)}, u32[]{:S(2)}) collective-permute-start(f32[128,256]{1,0:T(8,128)S(1)} %get-tuple-element.39), channel_id=1, source_target_pairs={{0,3},{1,0},{2,1},{3,2},{4,7},{5,4},{6,5},{7,6},{8,11},{9,8},{10,9... | collective-permute-start | bytes 393224 | tf_op jit(solution)/shard_map/ppermute | solution.py:21
  116.5 1.2 copy-start.1
  150.8 26.0 %all-to-all-start.2 = ((f32[4,8,1024]{2,1,0:T(8,128)}), f32[4,8,1024]{2,1,0:T(8,128)S(1)}, u32[]{:S(2)}, u32[]{:S(2)}) async-start(f32[4,8,1024]{2,1,0:T(8,128)} %bitcast.35), calls=%async_computation.2 | async-start | bytes 262144 | tf_op jit(solution)/shard_map/all_to_all | solution.py:25
  163.2 2.2 %copy-start.2 = (f32[4,128,256]{2,1,0:T(8,128)S(1)}, f32[4,128,256]{2,1,0:T(8,128)}, u32[]{:S(2)}) copy-start(f32[4,128,256]{2,1,0:T(8,128)} %copy-done.1) | copy-start | bytes 1572868
  165.4 32.8 %copy-start.5 = (f32[64,1024]{1,0:T(8,128)S(1)}, f32[64,1024]{1,0:T(8,128)}, u32[]{:S(2)}) copy-start(f32[64,1024]{1,0:T(8,128)} %param.10) | copy-start | bytes 786436
where the time goes:
time: 200 us; the launch traced here: 199 us
  blocking collectives  86.5 us (43%)
  starting transfers between devices  59.7 us (30%)
  waiting for transfers between devices  25.1 us (13%)
  matrix products  11.9 us (6%)
  other arithmetic  9.66 us (5%)
  local copies, waits for them, and re-layouts  4.85 us (2%)
    all_to_all x2, blocking collectives, exchanged(): return lax.all_to_all(blocks, axes, 0, 0, tiled=True)  65.1 us
    ppermute x14, starting transfers between devices, moved(): lax.ppermute(block, axis, [(i, (i + distance) % size) for i in range(size)])  47.2 us
    all_gather x1, blocking collectives, shards(): word_total = lax.all_gather(sums, ('zh', 'core'), tiled=True)  21.4 us
    ppermute x14, waiting for transfers between devices, moved(): lax.ppermute(block, axis, [(i, (i + distance) % size) for i in range(size)])  17.6 us
    all_to_all x1, starting transfers between devices, exchanged(): return lax.all_to_all(blocks, axes, 0, 0, tiled=True)  12.5 us
    dot_general x6, matrix products, matmul(): lax.dot_general(left, right, (contract, ((), ())), precision=lax.Precisio...  11.9 us
    all_to_all x1, waiting for transfers between devices, exchanged(): return lax.all_to_all(blocks, axes, 0, 0, tiled=True)  7.51 us
  transfers between devices with their start and end apart: 15, of which 6 were waited for; matrix products, arithmetic and copies ran while one was open for 9% of the time, Pallas kernels for 0%

commit v1 on v0

v1 whole, which is shorter than its diff:
```python
import jax
import jax.numpy as jnp
from jax import lax
from jax.sharding import Mesh, PartitionSpec as P


VOCAB = 1048576
ALPHA = 0.1
BETA = 0.01

CORES = 2
EXTRA = 8


def wrapped(place, size):
    return place & (size - 1)


def moved(block, axis, partner):
    return lax.ppermute(block, axis, [(i, partner(i)) for i in range(lax.axis_size(axis))])


def after(arrived, earlier):
    return lax.optimization_barrier((arrived, earlier))[0]


def exchanged(blocks, axes):
    return lax.all_to_all(blocks, axes, 0, 0, tiled=True)


def scattered(sums, axes):
    members = lax.axis_size(axes)
    rows = sums.shape[0] // members
    return jnp.sum(exchanged(sums, axes).reshape(members, rows, sums.shape[1]), axis=0)


def matmul(left, right, contract):
    return lax.dot_general(left, right, (contract, ((), ())), precision=lax.Precision.HIGH, preferred_element_type=jnp.float32)


def first_partner(i):
    return i ^ 1


def second_partner(i):
    return i ^ 2


def across(i):
    return 3 - i


def joined(own, other, place):
    both = lax.dynamic_update_index_in_dim(jnp.zeros((2,) + own.shape, own.dtype), own, place, 0)
    return lax.dynamic_update_index_in_dim(both, other, 1 - place, 0).reshape((2 * own.shape[0],) + own.shape[1:])


def shards(doc_mix, doc_lengths, counts, tile_on, word_counts, topic_totals):
    docs, topics = doc_mix.shape
    slice_words = word_counts.shape[0]
    n_zh, n_t = lax.axis_size("zh"), lax.axis_size("t")
    cut = ("y", "x")
    n_cuts = lax.axis_size(cut)
    core, t = lax.axis_index("core"), lax.axis_index("t")
    half = slice_words // CORES
    rows = half // n_zh
    chunk = n_cuts * half // n_t
    low, high = t & 1, t >> 1
    quarter = 2 * low + high

    scale = (topic_totals + VOCAB * BETA)[None, :]
    own_counts = lax.dynamic_index_in_dim(word_counts.reshape(n_zh, CORES, rows, topics), core, 1, False).reshape(half, topics)
    own_half = (own_counts + BETA) / scale
    copies = jnp.broadcast_to(own_half[None], (n_cuts, half, topics)).reshape(n_cuts * half, topics)
    words = [exchanged(copies, cut)]
    words.append(moved(words[0], "core", first_partner))

    chunk_cuts = n_cuts // n_t
    chunk_counts = lax.dynamic_slice_in_dim(counts, quarter * (chunk_cuts * slice_words), chunk_cuts * slice_words, 1)
    chunk_tiles = lax.dynamic_slice_in_dim(tile_on[0], quarter * chunk_cuts, chunk_cuts, 0)
    weights = (chunk_counts.T * jnp.repeat(chunk_tiles, slice_words)[:, None]).astype(jnp.float32)
    weights = weights.reshape(chunk_cuts, n_zh, CORES, rows, docs)

    def chunk_weights(wave):
        return lax.dynamic_index_in_dim(weights, wrapped(core + wave, CORES), 2, False).reshape(chunk, docs)

    def parts_of(wave, mix):
        products = matmul(words[wave], mix, ((1,), (1,)))
        word_sums = matmul(jnp.ones((EXTRA - 1, topics), jnp.float32), words[wave], ((1,), (1,)))
        span = 2 * chunk
        halves = []
        for h in range(2):
            sums = jnp.pad(word_sums[:, h * span : (h + 1) * span], ((0, 0), (0, docs - span)))
            halves.append(jnp.concatenate([products[h * span : (h + 1) * span], mass_part, sums], axis=0))
        both = jnp.stack(halves)
        return lax.dynamic_index_in_dim(both, low, 0, False), lax.dynamic_index_in_dim(both, 1 - low, 0, False)

    def split(kept):
        chunks, extra = kept[: 2 * chunk].reshape(2, chunk, docs), kept[2 * chunk :]
        return [jnp.concatenate([lax.dynamic_index_in_dim(chunks, i, 0, False), extra], axis=0) for i in (high, 1 - high)]

    def ratio_of(wave, total, doc_scale):
        word_sums = lax.dynamic_slice_in_dim(total[chunk + 1], high * chunk, chunk, 0)
        return chunk_weights(wave) / (total[:chunk] * doc_scale[None, :] + ALPHA * word_sums[:, None])

    mass_part = jnp.sum(doc_mix, axis=1)[None, :]
    own_0, given_0 = parts_of(0, doc_mix)
    arrived_0 = moved(given_0, "t", first_partner)
    own_1, given_1 = parts_of(1, after(doc_mix, given_0))
    arrived_1 = moved(given_1, "t", first_partner)

    own_0, given_0 = split(own_0 + after(arrived_0, given_1))
    arrived_0 = moved(given_0, "t", second_partner)
    own_1, given_1 = split(own_1 + after(arrived_1, given_0))
    arrived_1 = moved(given_1, "t", second_partner)

    total = own_0 + after(arrived_0, given_1)
    doc_scale = doc_lengths.astype(jnp.float32) / total[chunk]
    doc_weight = doc_mix * doc_scale[:, None] + ALPHA
    chunk_0 = ratio_of(0, total, doc_scale)
    arrived_0 = moved(chunk_0, "t", second_partner)
    total = own_1 + after(arrived_1, chunk_0)
    chunk_1 = ratio_of(1, total, doc_scale)
    arrived_1 = moved(chunk_1, "t", second_partner)

    half_0 = joined(chunk_0, after(arrived_0, chunk_1), high)
    arrived_0 = moved(half_0, "t", first_partner)
    half_1 = joined(chunk_1, after(arrived_1, half_0), high)
    arrived_1 = moved(half_1, "t", first_partner)

    by_doc = ((1,), (0,))
    ratio_0 = joined(half_0, after(arrived_0, half_1), low)
    sums_0 = matmul(ratio_0, doc_weight, by_doc)
    sums_given = moved(sums_0, "core", first_partner)
    ratio_1 = joined(half_1, after(arrived_1, sums_0), low)

    sums = scattered(matmul(ratio_1, doc_weight, by_doc) + sums_given, cut)
    own_a, own_b = lax.optimization_barrier((sums[: half // 2], sums[half // 2 :]))
    arrived_a = moved(own_a, "zh", first_partner)
    arrived_b = moved(own_b, "zh", first_partner)
    own_a = own_a + arrived_a
    arrived_a = moved(own_a, "zh", across)
    own_b = own_b + after(arrived_b, own_a)
    arrived_b = moved(own_b, "zh", across)
    own_total = jnp.concatenate([own_a + arrived_a, own_b + arrived_b], axis=0)
    other_total = moved(own_total, "core", first_partner)
    own_total, other_total = (v.reshape(n_zh, 1, rows, topics) for v in (own_total, other_total))
    pair = (jnp.concatenate([other_total, own_total], axis=1), jnp.concatenate([own_total, other_total], axis=1))
    word_total = jnp.where(core == 0, *pair).reshape(slice_words, topics)

    by_word = ((0,), (0,))
    doc_sums = matmul(ratio_0, words[0], by_word) + matmul(ratio_1, words[1], by_word)
    return (doc_weight * doc_sums, (word_counts + BETA) / scale * word_total)


def solution(mesh):
    dp, cuts, topic = (mesh.shape[a] for a in ("dp", "cuts", "topic"))
    side = int(round(cuts**0.5))
    finer = Mesh(mesh.devices.reshape(dp // CORES, CORES, cuts // side, side, topic), ("zh", "core", "y", "x", "t"))
    docs, cut = ("zh", "core", "y", "x"), ("y", "x")

    return jax.shard_map(
        shards,
        mesh=finer,
        in_specs=(P(docs, "t"), P(docs), P(docs, None), P(docs, None), P(cut, "t"), P("t")),
        out_specs=(P(docs, "t"), P(cut, "t")),
        check_vma=False,
    )
```

time: 200 us -> 191 us (0.955)
  blocking collectives: 86.5 us -> 64.3 us
  waiting for transfers between devices: 25.1 us -> 39.5 us
  matrix products: 11.9 us -> 19 us
  other arithmetic: 9.66 us -> 5.11 us
  local copies, waits for them, and re-layouts: 4.85 us -> 1.11 us
    ppermute x14 -> x15, waiting for transfers between devices: 17.6 us -> 39.5 us  [moved(): lax.ppermute(block, axis, [(i, partner(i)) for i in range(lax.axis_size(a...]
    all_gather x1 -> x0, blocking collectives: 21.4 us -> none  [shards(): word_total = lax.all_gather(sums, ('zh', 'core'), tiled=True)]
    ppermute x14 -> x15, starting transfers between devices: 47.2 us -> 59.8 us  [moved(): lax.ppermute(block, axis, [(i, partner(i)) for i in range(lax.axis_size(a...]
    all_to_all x1 -> x0, starting transfers between devices: 12.5 us -> none  [exchanged(): return lax.all_to_all(blocks, axes, 0, 0, tiled=True)]
    all_to_all x1 -> x0, waiting for transfers between devices: 7.51 us -> none  [exchanged(): return lax.all_to_all(blocks, axes, 0, 0, tiled=True)]
    dot_general x6 -> x8, matrix products: 11.9 us -> 19 us  [matmul(): lax.dot_general(left, right, (contract, ((), ())), precision=lax.Precisio...]
    unnamed x17 -> x11, local copies, waits for them, and re-layouts: 3.37 us -> 0.16 us
  transfers between devices with their start and end apart: 15 -> 15, of which waited for: 6 -> 8; matrix products, arithmetic and copies ran while one was open for 9% -> 10% of each run, Pallas kernels for 0% -> 0%
where the time goes in v1:
time: 191 us; the launch traced here: 190 us
  blocking collectives  64.3 us (34%)
  starting transfers between devices  59.8 us (31%)
  waiting for transfers between devices  39.5 us (21%)
  matrix products  19 us (10%)
  other arithmetic  5.11 us (3%)
    all_to_all x2, blocking collectives, exchanged(): return lax.all_to_all(blocks, axes, 0, 0, tiled=True)  64.3 us
    ppermute x15, starting transfers between devices, moved(): lax.ppermute(block, axis, [(i, partner(i)) for i in range(lax.axis_size(a...  59.8 us
    ppermute x15, waiting for transfers between devices, moved(): lax.ppermute(block, axis, [(i, partner(i)) for i in range(lax.axis_size(a...  39.5 us
    dot_general x8, matrix products, matmul(): lax.dot_general(left, right, (contract, ((), ())), precision=lax.Precisio...  19 us
  transfers between devices with their start and end apart: 15, of which 8 were waited for; matrix products, arithmetic and copies ran while one was open for 10% of the time, Pallas kernels for 0%

profile of v1, /device:TPU:1, one launch (start us, length us, event | category | flops | bytes accessed | tf_op | source)
XLA Modules:
  0.0 190.0 jit_solution(1881501541554209064)
XLA Ops:
  2.6 33.6 %all_to_all.18 = f32[16,32,1024]{2,1,0:T(8,128)} all-to-all(f32[16,32,1024]{2,1,0:T(8,128)S(1)} %broadcast_in_dim.44), channel_id=1, replica_groups=mesh['zh'=4,'core'=2,'y'=4,'x'=4,'t'=4] {'y','x'}, dimensions={0} | all-to-all | bytes 4194304 | tf_op jit(solution)/shard_map/all_to_all | solution.py:28
  36.2 5.5 %collective-permute-start.1 = (f32[512,1024]{1,0:T(8,128)}, f32[512,1024]{1,0:T(8,128)}, u32[]{:S(2)}, u32[]{:S(2)}) collective-permute-start(f32[512,1024]{1,0:T(8,128)} %bitcast.2), channel_id=1, source_target_pairs={{0,64},{64,0},{1,65},{65,1},{2,66},{66,2},{3,67},{67,3},{4,68},{68... | collective-permute-start | bytes 6291464 | tf_op jit(solution)/shard_map/ppermute | solution.py:20
  42.4 2.5 %fusion.32 = f32[7,512]{1,0:T(8,128)S(1)} fusion(f32[512,1024]{1,0:T(8,128)} %bitcast.2), kind=kOutput, calls=%fused_computation.70 | convolution fusion | flops 22020096 | bytes 2111488 | tf_op jit(solution)/shard_map/dot_general | solution.py:38
  44.9 2.6 %fusion.50 = f32[512,256]{1,0:T(8,128)S(1)} fusion(f32[512,1024]{1,0:T(8,128)} %bitcast.2, f32[256,1024]{1,0:T(8,128)S(1)} %copy-done.1), kind=kOutput, calls=%fused_computation.96 | convolution fusion | flops 805306368 | bytes 3670016 | tf_op jit(solution)/shard_map/dot_general | solution.py:38
  47.7 3.4 %collective-permute-start = (f32[264,256]{1,0:T(8,128)S(1)}, f32[264,256]{1,0:T(8,128)S(1)}, u32[]{:S(2)}, u32[]{:S(2)}) collective-permute-start(f32[264,256]{1,0:T(8,128)S(1)} %fusion.20), channel_id=1, source_target_pairs={{0,1},{1,0},{2,3},{3,2},{4,5},{5,4},{6,7},{7,6},{8,9},{9,8},{10,11... | collective-permute-start | bytes 811016 | tf_op jit(solution)/shard_map/ppermute | solution.py:20
  51.1 2.6 %fusion.51 = f32[512,256]{1,0:T(8,128)S(1)} fusion(f32[512,1024]{1,0:T(8,128)} %collective-permute-done.1, f32[256,1024]{1,0:T(8,128)S(1)} %copy-done.1), kind=kOutput, calls=%fused_computation.97 | convolution fusion | flops 805306368 | bytes 3670016 | tf_op jit(solution)/shard_map/dot_general | solution.py:38
  53.7 2.5 %fusion.30 = f32[7,512]{1,0:T(8,128)S(1)} fusion(f32[512,1024]{1,0:T(8,128)} %collective-permute-done.1), kind=kOutput, calls=%fused_computation.68 | convolution fusion | flops 22020096 | bytes 2111488 | tf_op jit(solution)/shard_map/dot_general | solution.py:38
  56.4 1.9 %collective-permute-start.3 = (f32[264,256]{1,0:T(8,128)S(1)}, f32[264,256]{1,0:T(8,128)S(1)}, u32[]{:S(2)}, u32[]{:S(2)}) collective-permute-start(f32[264,256]{1,0:T(8,128)S(1)} %fusion.18), channel_id=1, source_target_pairs={{0,1},{1,0},{2,3},{3,2},{4,5},{5,4},{6,7},{7,6},{8,9},{9,8},{10,11... | collective-permute-start | bytes 811016 | tf_op jit(solution)/shard_map/ppermute | solution.py:20
  58.5 4.9 %collective-permute-start.2 = (f32[136,256]{1,0:T(8,128)S(1)}, f32[136,256]{1,0:T(8,128)S(1)}, u32[]{:S(2)}, u32[]{:S(2)}) collective-permute-start(f32[136,256]{1,0:T(8,128)S(1)} %pad_maximum_fusion.4), channel_id=1, source_target_pairs={{0,2},{1,3},{2,0},{3,1},{4,6},{5,7},{6,4},{7,5},{8,10},{9,11},{10,... | collective-permute-start | bytes 417800 | tf_op jit(solution)/shard_map/ppermute | solution.py:20
  63.4 5.6 %collective-permute-done.3 = f32[264,256]{1,0:T(8,128)S(1)} collective-permute-done((f32[264,256]{1,0:T(8,128)S(1)}, f32[264,256]{1,0:T(8,128)S(1)}, u32[]{:S(2)}, u32[]{:S(2)}) %collective-permute-start.3) | collective-permute-done | bytes 270368 | tf_op jit(solution)/shard_map/ppermute | solution.py:20
  69.2 1.9 %collective-permute-start.5 = (f32[136,256]{1,0:T(8,128)S(1)}, f32[136,256]{1,0:T(8,128)S(1)}, u32[]{:S(2)}, u32[]{:S(2)}) collective-permute-start(f32[136,256]{1,0:T(8,128)S(1)} %pad_maximum_fusion.7), channel_id=1, source_target_pairs={{0,2},{1,3},{2,0},{3,1},{4,6},{5,7},{6,4},{7,5},{8,10},{9,11},{10,... | collective-permute-start | bytes 417800 | tf_op jit(solution)/shard_map/ppermute | solution.py:20
  71.3 4.3 %collective-permute-start.4 = (f32[128,256]{1,0:T(8,128)S(1)}, f32[128,256]{1,0:T(8,128)S(1)}, u32[]{:S(2)}, u32[]{:S(2)}) collective-permute-start(f32[128,256]{1,0:T(8,128)S(1)} %get-tuple-element.51), channel_id=1, source_target_pairs={{0,2},{1,3},{2,0},{3,1},{4,6},{5,7},{6,4},{7,5},{8,10},{9,11},{10,... | collective-permute-start | bytes 393224 | tf_op jit(solution)/shard_map/ppermute | solution.py:20
  75.6 6.7 %collective-permute-done.5 = f32[136,256]{1,0:T(8,128)S(1)} collective-permute-done((f32[136,256]{1,0:T(8,128)S(1)}, f32[136,256]{1,0:T(8,128)S(1)}, u32[]{:S(2)}, u32[]{:S(2)}) %collective-permute-start.5) | collective-permute-done | bytes 139296 | tf_op jit(solution)/shard_map/ppermute | solution.py:20
  82.5 1.9 %collective-permute-start.7 = (f32[128,256]{1,0:T(8,128)S(1)}, f32[128,256]{1,0:T(8,128)S(1)}, u32[]{:S(2)}, u32[]{:S(2)}) collective-permute-start(f32[128,256]{1,0:T(8,128)S(1)} %get-tuple-element.53), channel_id=1, source_target_pairs={{0,2},{1,3},{2,0},{3,1},{4,6},{5,7},{6,4},{7,5},{8,10},{9,11},{10,... | collective-permute-start | bytes 393224 | tf_op jit(solution)/shard_map/ppermute | solution.py:20
  85.1 2.8 %collective-permute-start.6 = (f32[256,256]{1,0:T(8,128)S(1)}, f32[256,256]{1,0:T(8,128)S(1)}, u32[]{:S(2)}, u32[]{:S(2)}) collective-permute-start(f32[256,256]{1,0:T(8,128)S(1)} %bitcast.96), channel_id=1, source_target_pairs={{0,1},{1,0},{2,3},{3,2},{4,5},{5,4},{6,7},{7,6},{8,9},{9,8},{10,11... | collective-permute-start | bytes 786440 | tf_op jit(solution)/shard_map/ppermute | solution.py:20
  88.0 4.5 %collective-permute-done.7 = f32[128,256]{1,0:T(8,128)S(1)} collective-permute-done((f32[128,256]{1,0:T(8,128)S(1)}, f32[128,256]{1,0:T(8,128)S(1)}, u32[]{:S(2)}, u32[]{:S(2)}) %collective-permute-start.7) | collective-permute-done | bytes 131104 | tf_op jit(solution)/shard_map/ppermute | solution.py:20
  92.5 5.3 %collective-permute-done.6 = f32[256,256]{1,0:T(8,128)S(1)} collective-permute-done((f32[256,256]{1,0:T(8,128)S(1)}, f32[256,256]{1,0:T(8,128)S(1)}, u32[]{:S(2)}, u32[]{:S(2)}) %collective-permute-start.6) | collective-permute-done | bytes 262176 | tf_op jit(solution)/shard_map/ppermute | solution.py:20
  99.0 2.5 %collective-permute-start.9 = (f32[512,1024]{1,0:T(8,128)S(1)}, f32[512,1024]{1,0:T(8,128)S(1)}, u32[]{:S(2)}, u32[]{:S(2)}) collective-permute-start(f32[512,1024]{1,0:T(8,128)S(1)} %fusion.1), channel_id=1, source_target_pairs={{0,64},{64,0},{1,65},{65,1},{2,66},{66,2},{3,67},{67,3},{4,68},{68... | collective-permute-start | bytes 6291464 | tf_op jit(solution)/shard_map/ppermute | solution.py:20
  101.6 1.9 %collective-permute-start.8 = (f32[256,256]{1,0:T(8,128)S(1)}, f32[256,256]{1,0:T(8,128)S(1)}, u32[]{:S(2)}, u32[]{:S(2)}) collective-permute-start(f32[256,256]{1,0:T(8,128)S(1)} %bitcast.94), channel_id=1, source_target_pairs={{0,1},{1,0},{2,3},{3,2},{4,5},{5,4},{6,7},{7,6},{8,9},{9,8},{10,11... | collective-permute-start | bytes 786440 | tf_op jit(solution)/shard_map/ppermute | solution.py:20
  103.6 7.7 %collective-permute-done.8 = f32[256,256]{1,0:T(8,128)S(1)} collective-permute-done((f32[256,256]{1,0:T(8,128)S(1)}, f32[256,256]{1,0:T(8,128)S(1)}, u32[]{:S(2)}, u32[]{:S(2)}) %collective-permute-start.8) | collective-permute-done | bytes 262176 | tf_op jit(solution)/shard_map/ppermute | solution.py:20
  111.4 1.2 convolution_add_fusion
  112.5 30.7 %all_to_all.19 = f32[16,32,1024]{2,1,0:T(8,128)} all-to-all(f32[16,32,1024]{2,1,0:T(8,128)S(1)} %bitcast.89), channel_id=1, replica_groups=mesh['zh'=4,'core'=2,'y'=4,'x'=4,'t'=4] {'y','x'}, dimensions={0} | all-to-all | bytes 4194304 | tf_op jit(solution)/shard_map/all_to_all | solution.py:28
  143.2 1.7 reduce_sum.19
  145.0 8.8 %collective-permute-start.10 = (f32[16,1024]{1,0:T(8,128)S(1)}, f32[16,1024]{1,0:T(8,128)S(1)}, u32[]{:S(2)}, u32[]{:S(2)}) collective-permute-start(f32[16,1024]{1,0:T(8,128)S(1)} %get-tuple-element.23), channel_id=1, source_target_pairs={{0,128},{128,0},{256,384},{384,256},{1,129},{129,1},{257,385},{385... | collective-permute-start | bytes 196616 | tf_op jit(solution)/shard_map/ppermute | solution.py:20
  153.7 1.9 %collective-permute-start.12 = (f32[16,1024]{1,0:T(8,128)S(1)}, f32[16,1024]{1,0:T(8,128)S(1)}, u32[]{:S(2)}, u32[]{:S(2)}) collective-permute-start(f32[16,1024]{1,0:T(8,128)S(1)} %get-tuple-element.24), channel_id=1, source_target_pairs={{0,128},{128,0},{256,384},{384,256},{1,129},{129,1},{257,385},{385... | collective-permute-start | bytes 196616 | tf_op jit(solution)/shard_map/ppermute | solution.py:20
  155.7 4.5 %collective-permute-done.10 = f32[16,1024]{1,0:T(8,128)S(1)} collective-permute-done((f32[16,1024]{1,0:T(8,128)S(1)}, f32[16,1024]{1,0:T(8,128)S(1)}, u32[]{:S(2)}, u32[]{:S(2)}) %collective-permute-start.10) | collective-permute-done | bytes 65568 | tf_op jit(solution)/shard_map/ppermute | solution.py:20
  160.2 11.6 %collective-permute-start.11 = (f32[16,1024]{1,0:T(8,128)S(1)}, f32[16,1024]{1,0:T(8,128)S(1)}, u32[]{:S(2)}, u32[]{:S(2)}) collective-permute-start(f32[16,1024]{1,0:T(8,128)S(1)} %add.165), channel_id=1, source_target_pairs={{0,384},{128,256},{256,128},{384,0},{1,385},{129,257},{257,129},{3... | collective-permute-start | bytes 196616 | tf_op jit(solution)/shard_map/ppermute | solution.py:20
  171.9 1.9 %collective-permute-start.13 = (f32[16,1024]{1,0:T(8,128)S(1)}, f32[16,1024]{1,0:T(8,128)S(1)}, u32[]{:S(2)}, u32[]{:S(2)}) collective-permute-start(f32[16,1024]{1,0:T(8,128)S(1)} %add.167), channel_id=1, source_target_pairs={{0,384},{128,256},{256,128},{384,0},{1,385},{129,257},{257,129},{3... | collective-permute-start | bytes 196616 | tf_op jit(solution)/shard_map/ppermute | solution.py:20
  173.8 2.7 %fusion.52 = f32[256,1024]{1,0:T(8,128)S(1)} fusion(f32[512,256]{1,0:T(8,128)S(1)} %bitcast.93, f32[512,1024]{1,0:T(8,128)} %bitcast.2), kind=kOutput, calls=%fused_computation.98 | convolution fusion | flops 805306368 | bytes 3670016 | tf_op jit(solution)/shard_map/dot_general | solution.py:38
  176.5 4.3 %collective-permute-done.13 = f32[16,1024]{1,0:T(8,128)S(1)} collective-permute-done((f32[16,1024]{1,0:T(8,128)S(1)}, f32[16,1024]{1,0:T(8,128)S(1)}, u32[]{:S(2)}, u32[]{:S(2)}) %collective-permute-start.13) | collective-permute-done | bytes 65568 | tf_op jit(solution)/shard_map/ppermute | solution.py:20
  180.9 4.6 %collective-permute-start.14 = (f32[32,1024]{1,0:T(8,128)S(1)}, f32[32,1024]{1,0:T(8,128)S(1)}, u32[]{:S(2)}, u32[]{:S(2)}) collective-permute-start(f32[32,1024]{1,0:T(8,128)S(1)} %get-tuple-element.38), channel_id=1, source_target_pairs={{0,64},{64,0},{1,65},{65,1},{2,66},{66,2},{3,67},{67,3},{4,68},{68... | collective-permute-start | bytes 393224 | tf_op jit(solution)/shard_map/ppermute | solution.py:20
  185.5 3.7 %fusion = f32[256,1024]{1,0:T(8,128)} fusion(f32[256,1024]{1,0:T(8,128)S(1)} %fusion.52, f32[512,256]{1,0:T(8,128)S(1)} %bitcast.91, f32[512,1024]{1,0:T(8,128)} %collective-permute-done.1, f32[256,1024]{1,0:T(8,128)S(1)} %copy-done.1, f32[256]{0:T(256)S(1)} %convert_divide_fusion), kind=kOutput, calls=%fused_computation.2 | convolution fusion | flops 806354944 | bytes 5768192 | tf_op jit(solution)/shard_map/dot_general | solution.py:38
  (75 shorter events, 6.4 us)
Async XLA Ops:
  0.6 41.0 %copy-start = (s32[256,1024]{1,0:T(8,128)S(1)}, s32[256,1024]{1,0:T(8,128)}, u32[]{:S(2)}) copy-start(s32[256,1024]{1,0:T(8,128)} %param.8) | copy-start | bytes 3145732
  2.6 39.3 %copy-start.4 = (s32[1,16]{1,0:T(1,128)S(1)}, s32[1,16]{1,0:T(1,128)}, u32[]{:S(2)}) copy-start(s32[1,16]{1,0:T(1,128)} %param.9) | copy-start | bytes 196
  2.6 39.5 %copy-start.1 = (f32[256,1024]{1,0:T(8,128)S(1)}, f32[256,1024]{1,0:T(8,128)}, u32[]{:S(2)}) copy-start(f32[256,1024]{1,0:T(8,128)} %param.6) | copy-start | bytes 3145732
  36.2 14.9 %collective-permute-start.1 = (f32[512,1024]{1,0:T(8,128)}, f32[512,1024]{1,0:T(8,128)}, u32[]{:S(2)}, u32[]{:S(2)}) collective-permute-start(f32[512,1024]{1,0:T(8,128)} %bitcast.2), channel_id=1, source_target_pairs={{0,64},{64,0},{1,65},{65,1},{2,66},{66,2},{3,67},{67,3},{4,68},{68... | collective-permute-start | bytes 6291464 | tf_op jit(solution)/shard_map/ppermute | solution.py:20
  47.7 10.6 %collective-permute-start = (f32[264,256]{1,0:T(8,128)S(1)}, f32[264,256]{1,0:T(8,128)S(1)}, u32[]{:S(2)}, u32[]{:S(2)}) collective-permute-start(f32[264,256]{1,0:T(8,128)S(1)} %fusion.20), channel_id=1, source_target_pairs={{0,1},{1,0},{2,3},{3,2},{4,5},{5,4},{6,7},{7,6},{8,9},{9,8},{10,11... | collective-permute-start | bytes 811016 | tf_op jit(solution)/shard_map/ppermute | solution.py:20
  56.4 12.6 %collective-permute-start.3 = (f32[264,256]{1,0:T(8,128)S(1)}, f32[264,256]{1,0:T(8,128)S(1)}, u32[]{:S(2)}, u32[]{:S(2)}) collective-permute-start(f32[264,256]{1,0:T(8,128)S(1)} %fusion.18), channel_id=1, source_target_pairs={{0,1},{1,0},{2,3},{3,2},{4,5},{5,4},{6,7},{7,6},{8,9},{9,8},{10,11... | collective-permute-start | bytes 811016 | tf_op jit(solution)/shard_map/ppermute | solution.py:20
  58.4 12.8 %copy-start.3 = (s32[256]{0:T(256)S(1)}, s32[256]{0:T(256)}, u32[]{:S(2)}) copy-start(s32[256]{0:T(256)} %param.7) | copy-start | bytes 3076
  58.5 12.6 %collective-permute-start.2 = (f32[136,256]{1,0:T(8,128)S(1)}, f32[136,256]{1,0:T(8,128)S(1)}, u32[]{:S(2)}, u32[]{:S(2)}) collective-permute-start(f32[136,256]{1,0:T(8,128)S(1)} %pad_maximum_fusion.4), channel_id=1, source_target_pairs={{0,2},{1,3},{2,0},{3,1},{4,6},{5,7},{6,4},{7,5},{8,10},{9,11},{10,... | collective-permute-start | bytes 417800 | tf_op jit(solution)/shard_map/ppermute | solution.py:20
  69.2 13.1 %collective-permute-start.5 = (f32[136,256]{1,0:T(8,128)S(1)}, f32[136,256]{1,0:T(8,128)S(1)}, u32[]{:S(2)}, u32[]{:S(2)}) collective-permute-start(f32[136,256]{1,0:T(8,128)S(1)} %pad_maximum_fusion.7), channel_id=1, source_target_pairs={{0,2},{1,3},{2,0},{3,1},{4,6},{5,7},{6,4},{7,5},{8,10},{9,11},{10,... | collective-permute-start | bytes 417800 | tf_op jit(solution)/shard_map/ppermute | solution.py:20
  71.3 13.8 %collective-permute-start.4 = (f32[128,256]{1,0:T(8,128)S(1)}, f32[128,256]{1,0:T(8,128)S(1)}, u32[]{:S(2)}, u32[]{:S(2)}) collective-permute-start(f32[128,256]{1,0:T(8,128)S(1)} %get-tuple-element.51), channel_id=1, source_target_pairs={{0,2},{1,3},{2,0},{3,1},{4,6},{5,7},{6,4},{7,5},{8,10},{9,11},{10,... | collective-permute-start | bytes 393224 | tf_op jit(solution)/shard_map/ppermute | solution.py:20
  82.5 10.0 %collective-permute-start.7 = (f32[128,256]{1,0:T(8,128)S(1)}, f32[128,256]{1,0:T(8,128)S(1)}, u32[]{:S(2)}, u32[]{:S(2)}) collective-permute-start(f32[128,256]{1,0:T(8,128)S(1)} %get-tuple-element.53), channel_id=1, source_target_pairs={{0,2},{1,3},{2,0},{3,1},{4,6},{5,7},{6,4},{7,5},{8,10},{9,11},{10,... | collective-permute-start | bytes 393224 | tf_op jit(solution)/shard_map/ppermute | solution.py:20
  85.1 12.7 %collective-permute-start.6 = (f32[256,256]{1,0:T(8,128)S(1)}, f32[256,256]{1,0:T(8,128)S(1)}, u32[]{:S(2)}, u32[]{:S(2)}) collective-permute-start(f32[256,256]{1,0:T(8,128)S(1)} %bitcast.96), channel_id=1, source_target_pairs={{0,1},{1,0},{2,3},{3,2},{4,5},{5,4},{6,7},{7,6},{8,9},{9,8},{10,11... | collective-permute-start | bytes 786440 | tf_op jit(solution)/shard_map/ppermute | solution.py:20
  99.0 12.3 %collective-permute-start.9 = (f32[512,1024]{1,0:T(8,128)S(1)}, f32[512,1024]{1,0:T(8,128)S(1)}, u32[]{:S(2)}, u32[]{:S(2)}) collective-permute-start(f32[512,1024]{1,0:T(8,128)S(1)} %fusion.1), channel_id=1, source_target_pairs={{0,64},{64,0},{1,65},{65,1},{2,66},{66,2},{3,67},{67,3},{4,68},{68... | collective-permute-start | bytes 6291464 | tf_op jit(solution)/shard_map/ppermute | solution.py:20
  101.6 9.7 %collective-permute-start.8 = (f32[256,256]{1,0:T(8,128)S(1)}, f32[256,256]{1,0:T(8,128)S(1)}, u32[]{:S(2)}, u32[]{:S(2)}) collective-permute-start(f32[256,256]{1,0:T(8,128)S(1)} %bitcast.94), channel_id=1, source_target_pairs={{0,1},{1,0},{2,3},{3,2},{4,5},{5,4},{6,7},{7,6},{8,9},{9,8},{10,11... | collective-permute-start | bytes 786440 | tf_op jit(solution)/shard_map/ppermute | solution.py:20
  145.0 15.2 %collective-permute-start.10 = (f32[16,1024]{1,0:T(8,128)S(1)}, f32[16,1024]{1,0:T(8,128)S(1)}, u32[]{:S(2)}, u32[]{:S(2)}) collective-permute-start(f32[16,1024]{1,0:T(8,128)S(1)} %get-tuple-element.23), channel_id=1, source_target_pairs={{0,128},{128,0},{256,384},{384,256},{1,129},{129,1},{257,385},{385... | collective-permute-start | bytes 196616 | tf_op jit(solution)/shard_map/ppermute | solution.py:20
  153.7 18.1 %collective-permute-start.12 = (f32[16,1024]{1,0:T(8,128)S(1)}, f32[16,1024]{1,0:T(8,128)S(1)}, u32[]{:S(2)}, u32[]{:S(2)}) collective-permute-start(f32[16,1024]{1,0:T(8,128)S(1)} %get-tuple-element.24), channel_id=1, source_target_pairs={{0,128},{128,0},{256,384},{384,256},{1,129},{129,1},{257,385},{385... | collective-permute-start | bytes 196616 | tf_op jit(solution)/shard_map/ppermute | solution.py:20
  160.2 20.6 %collective-permute-start.11 = (f32[16,1024]{1,0:T(8,128)S(1)}, f32[16,1024]{1,0:T(8,128)S(1)}, u32[]{:S(2)}, u32[]{:S(2)}) collective-permute-start(f32[16,1024]{1,0:T(8,128)S(1)} %add.165), channel_id=1, source_target_pairs={{0,384},{128,256},{256,128},{384,0},{1,385},{129,257},{257,129},{3... | collective-permute-start | bytes 196616 | tf_op jit(solution)/shard_map/ppermute | solution.py:20
  171.9 8.9 %collective-permute-start.13 = (f32[16,1024]{1,0:T(8,128)S(1)}, f32[16,1024]{1,0:T(8,128)S(1)}, u32[]{:S(2)}, u32[]{:S(2)}) collective-permute-start(f32[16,1024]{1,0:T(8,128)S(1)} %add.167), channel_id=1, source_target_pairs={{0,384},{128,256},{256,128},{384,0},{1,385},{129,257},{257,129},{3... | collective-permute-start | bytes 196616 | tf_op jit(solution)/shard_map/ppermute | solution.py:20
  180.9 8.4 %copy-start.2 = (f32[64,1024]{1,0:T(8,128)S(1)}, f32[64,1024]{1,0:T(8,128)}, u32[]{:S(2)}) copy-start(f32[64,1024]{1,0:T(8,128)} %param.10) | copy-start | bytes 786436
  180.9 8.4 %collective-permute-start.14 = (f32[32,1024]{1,0:T(8,128)S(1)}, f32[32,1024]{1,0:T(8,128)S(1)}, u32[]{:S(2)}, u32[]{:S(2)}) collective-permute-start(f32[32,1024]{1,0:T(8,128)S(1)} %get-tuple-element.38), channel_id=1, source_target_pairs={{0,64},{64,0},{1,65},{65,1},{2,66},{66,2},{3,67},{67,3},{4,68},{68... | collective-permute-start | bytes 393224 | tf_op jit(solution)/shard_map/ppermute | solution.py:20

commit v2 on v1

--- a/solution.py
+++ b/solution.py
@@ -85,22 +85,17 @@
         return lax.dynamic_index_in_dim(weights, wrapped(core + wave, CORES), 2, False).reshape(chunk, docs)
 
     def parts_of(wave, mix):
-        products = matmul(words[wave], mix, ((1,), (1,)))
-        word_sums = matmul(jnp.ones((EXTRA - 1, topics), jnp.float32), words[wave], ((1,), (1,)))
-        span = 2 * chunk
-        halves = []
-        for h in range(2):
-            sums = jnp.pad(word_sums[:, h * span : (h + 1) * span], ((0, 0), (0, docs - span)))
-            halves.append(jnp.concatenate([products[h * span : (h + 1) * span], mass_part, sums], axis=0))
-        both = jnp.stack(halves)
-        return lax.dynamic_index_in_dim(both, low, 0, False), lax.dynamic_index_in_dim(both, 1 - low, 0, False)
+        products = matmul(words[wave], mix, ((1,), (1,))).reshape(n_t, chunk, docs)
+        word_sums = jnp.sum(words[wave].reshape(n_cuts, half, topics), axis=2).reshape(n_t, 1, chunk)
+        word_sums = jnp.pad(word_sums, ((0, 0), (0, EXTRA - 2), (0, docs - chunk)))
+        parts = jnp.concatenate([products, jnp.broadcast_to(mass_part[None], (n_t, 1, docs)), word_sums], axis=1)
+        return picked(parts.reshape(2, n_t // 2, chunk + EXTRA, docs), low)
 
-    def split(kept):
-        chunks, extra = kept[: 2 * chunk].reshape(2, chunk, docs), kept[2 * chunk :]
-        return [jnp.concatenate([lax.dynamic_index_in_dim(chunks, i, 0, False), extra], axis=0) for i in (high, 1 - high)]
+    def picked(pair, place):
+        return lax.dynamic_index_in_dim(pair, place, 0, False), lax.dynamic_index_in_dim(pair, 1 - place, 0, False)
 
     def ratio_of(wave, total, doc_scale):
-        word_sums = lax.dynamic_slice_in_dim(total[chunk + 1], high * chunk, chunk, 0)
+        word_sums = total[chunk + 1, :chunk]
         return chunk_weights(wave) / (total[:chunk] * doc_scale[None, :] + ALPHA * word_sums[:, None])
 
     mass_part = jnp.sum(doc_mix, axis=1)[None, :]
@@ -109,9 +104,9 @@
     own_1, given_1 = parts_of(1, after(doc_mix, given_0))
     arrived_1 = moved(given_1, "t", first_partner)
 
-    own_0, given_0 = split(own_0 + after(arrived_0, given_1))
+    own_0, given_0 = picked(own_0 + after(arrived_0, given_1), high)
     arrived_0 = moved(given_0, "t", second_partner)
-    own_1, given_1 = split(own_1 + after(arrived_1, given_0))
+    own_1, given_1 = picked(own_1 + after(arrived_1, given_0), high)
     arrived_1 = moved(given_1, "t", second_partner)
 
     total = own_0 + after(arrived_0, given_1)
@@ -132,25 +127,26 @@
     ratio_0 = joined(half_0, after(arrived_0, half_1), low)
     sums_0 = matmul(ratio_0, doc_weight, by_doc)
     sums_given = moved(sums_0, "core", first_partner)
-    ratio_1 = joined(half_1, after(arrived_1, sums_0), low)
+    by_word = ((0,), (0,))
+    doc_sums = matmul(ratio_0, words[0], by_word)
+    ratio_1 = joined(half_1, after(arrived_1, doc_sums), low)
 
     sums = scattered(matmul(ratio_1, doc_weight, by_doc) + sums_given, cut)
     own_a, own_b = lax.optimization_barrier((sums[: half // 2], sums[half // 2 :]))
     arrived_a = moved(own_a, "zh", first_partner)
-    arrived_b = moved(own_b, "zh", first_partner)
-    own_a = own_a + arrived_a
+    arrived_b = moved(own_b, "zh", across)
+    doc_topic = doc_weight * (doc_sums + matmul(ratio_1, words[1], by_word))
+    own_a = own_a + after(arrived_a, doc_topic)
     arrived_a = moved(own_a, "zh", across)
     own_b = own_b + after(arrived_b, own_a)
-    arrived_b = moved(own_b, "zh", across)
+    arrived_b = moved(own_b, "zh", first_partner)
     own_total = jnp.concatenate([own_a + arrived_a, own_b + arrived_b], axis=0)
     other_total = moved(own_total, "core", first_partner)
     own_total, other_total = (v.reshape(n_zh, 1, rows, topics) for v in (own_total, other_total))
     pair = (jnp.concatenate([other_total, own_total], axis=1), jnp.concatenate([own_total, other_total], axis=1))
     word_total = jnp.where(core == 0, *pair).reshape(slice_words, topics)
 
-    by_word = ((0,), (0,))
-    doc_sums = matmul(ratio_0, words[0], by_word) + matmul(ratio_1, words[1], by_word)
-    return (doc_weight * doc_sums, (word_counts + BETA) / scale * word_total)
+    return (doc_topic, (word_counts + BETA) / scale * word_total)
 
 
 def solution(mesh):

time: 191 us -> 190 us (level)
  waiting for transfers between devices: 39.5 us -> 23.8 us
  starting transfers between devices: 59.8 us -> 74 us
  other arithmetic: 5.11 us -> 9.36 us
  matrix products: 19 us -> 15.1 us
    ppermute x15, waiting for transfers between devices: 39.5 us -> 23.8 us  [moved(): lax.ppermute(block, axis, [(i, partner(i)) for i in range(lax.axis_size(a...]
    ppermute x15, starting transfers between devices: 59.8 us -> 74 us  [moved(): lax.ppermute(block, axis, [(i, partner(i)) for i in range(lax.axis_size(a...]
    dot_general x8 -> x6, matrix products: 19 us -> 15.1 us  [matmul(): lax.dot_general(left, right, (contract, ((), ())), precision=lax.Precisio...]
    reduce_sum x0 -> x2, other arithmetic: none -> 3.53 us  [parts_of(): jnp.sum(words[wave].reshape(n_cuts, half, topics), axis=2)]
  transfers between devices with their start and end apart: 15 -> 15, of which waited for: 8 -> 9; matrix products, arithmetic and copies ran while one was open for 10% -> 10% of each run, Pallas kernels for 0% -> 0%
where the time goes in v2:
time: 190 us
  starting transfers between devices  74 us (39%)
  blocking collectives  64.3 us (34%)
  waiting for transfers between devices  23.8 us (13%)
  matrix products  15.1 us (8%)
  other arithmetic  9.36 us (5%)
    ppermute x15, starting transfers between devices, moved(): lax.ppermute(block, axis, [(i, partner(i)) for i in range(lax.axis_size(a...  74 us
    all_to_all x2, blocking collectives, exchanged(): return lax.all_to_all(blocks, axes, 0, 0, tiled=True)  64.3 us
    ppermute x15, waiting for transfers between devices, moved(): lax.ppermute(block, axis, [(i, partner(i)) for i in range(lax.axis_size(a...  23.8 us
    dot_general x6, matrix products, matmul(): lax.dot_general(left, right, (contract, ((), ())), precision=lax.Precisio...  15.1 us
  transfers between devices with their start and end apart: 15, of which 9 were waited for; matrix products, arithmetic and copies ran while one was open for 10% of the time, Pallas kernels for 0%

profile of v2, /device:TPU:1, one launch (start us, length us, event | category | flops | bytes accessed | tf_op | source)
XLA Modules:
  0.0 189.6 jit_solution(8159320061726781707)
XLA Ops:
  2.6 33.6 %all_to_all.18 = f32[16,32,1024]{2,1,0:T(8,128)} all-to-all(f32[16,32,1024]{2,1,0:T(8,128)S(1)} %broadcast_in_dim.49), channel_id=1, replica_groups=mesh['zh'=4,'core'=2,'y'=4,'x'=4,'t'=4] {'y','x'}, dimensions={0} | all-to-all | bytes 4194304 | tf_op jit(solution)/shard_map/all_to_all | solution.py:28
  36.2 5.4 %collective-permute-start.1 = (f32[512,1024]{1,0:T(8,128)}, f32[512,1024]{1,0:T(8,128)}, u32[]{:S(2)}, u32[]{:S(2)}) collective-permute-start(f32[512,1024]{1,0:T(8,128)} %bitcast.7), channel_id=1, source_target_pairs={{0,64},{64,0},{1,65},{65,1},{2,66},{66,2},{3,67},{67,3},{4,68},{68... | collective-permute-start | bytes 6291464 | tf_op jit(solution)/shard_map/ppermute | solution.py:20
  42.4 1.8 reduce_sum.37
  44.2 2.6 %fusion.1 = f32[4,128,256]{2,1,0:T(8,128)S(1)} fusion(f32[4,128,1024]{2,1,0:T(8,128)} %bitcast.2, f32[256,1024]{1,0:T(8,128)S(1)} %copy-done.1), kind=kOutput, calls=%fused_computation.3 | convolution fusion | flops 805306368 | bytes 3670016 | tf_op jit(solution)/shard_map/dot_general | solution.py:38
  47.6 3.4 %collective-permute-start = (f32[2,136,256]{2,1,0:T(8,128)}, f32[2,136,256]{2,1,0:T(8,128)}, u32[]{:S(2)}, u32[]{:S(2)}) collective-permute-start(f32[2,136,256]{2,1,0:T(8,128)} %dynamic-slice_bitcast_fusion.1), channel_id=1, source_target_pairs={{0,1},{1,0},{2,3},{3,2},{4,5},{5,4},{6,7},{7,6},{8,9},{9,8},{10,11... | collective-permute-start | bytes 835592 | tf_op jit(solution)/shard_map/ppermute | solution.py:20
  51.0 2.6 %fusion.19 = f32[512,256]{1,0:T(8,128)S(1)} fusion(f32[512,1024]{1,0:T(8,128)} %collective-permute-done.1, f32[256,1024]{1,0:T(8,128)S(1)} %copy-done.1), kind=kOutput, calls=%fused_computation.56 | convolution fusion | flops 805306368 | bytes 3670016 | tf_op jit(solution)/shard_map/dot_general | solution.py:38
  53.6 1.8 reduce_sum.38
  55.5 1.9 %collective-permute-start.3 = (f32[2,136,256]{2,1,0:T(8,128)S(1)}, f32[2,136,256]{2,1,0:T(8,128)S(1)}, u32[]{:S(2)}, u32[]{:S(2)}) collective-permute-start(f32[2,136,256]{2,1,0:T(8,128)S(1)} %dynamic-slice_bitcast_fusion), channel_id=1, source_target_pairs={{0,1},{1,0},{2,3},{3,2},{4,5},{5,4},{6,7},{7,6},{8,9},{9,8},{10,11... | collective-permute-start | bytes 835592 | tf_op jit(solution)/shard_map/ppermute | solution.py:20
  59.1 5.1 %collective-permute-start.2 = (f32[136,256]{1,0:T(8,128)S(1)}, f32[136,256]{1,0:T(8,128)S(1)}, u32[]{:S(2)}, u32[]{:S(2)}) collective-permute-start(f32[136,256]{1,0:T(8,128)S(1)} %dynamic-slice_bitcast_fusion.3), channel_id=1, source_target_pairs={{0,2},{1,3},{2,0},{3,1},{4,6},{5,7},{6,4},{7,5},{8,10},{9,11},{10,... | collective-permute-start | bytes 417800 | tf_op jit(solution)/shard_map/ppermute | solution.py:20
  64.2 1.2 collective-permute-done.3
  65.4 2.1 %collective-permute-done.2 = f32[136,256]{1,0:T(8,128)S(1)} collective-permute-done((f32[136,256]{1,0:T(8,128)S(1)}, f32[136,256]{1,0:T(8,128)S(1)}, u32[]{:S(2)}, u32[]{:S(2)}) %collective-permute-start.2) | collective-permute-done | bytes 139296 | tf_op jit(solution)/shard_map/ppermute | solution.py:20
  67.6 4.0 %collective-permute-start.5 = (f32[136,256]{1,0:T(8,128)S(1)}, f32[136,256]{1,0:T(8,128)S(1)}, u32[]{:S(2)}, u32[]{:S(2)}) collective-permute-start(f32[136,256]{1,0:T(8,128)S(1)} %dynamic-slice_bitcast_fusion.2), channel_id=1, source_target_pairs={{0,2},{1,3},{2,0},{3,1},{4,6},{5,7},{6,4},{7,5},{8,10},{9,11},{10,... | collective-permute-start | bytes 417800 | tf_op jit(solution)/shard_map/ppermute | solution.py:20
  71.7 2.2 %collective-permute-start.4 = (f32[128,256]{1,0:T(8,128)S(1)}, f32[128,256]{1,0:T(8,128)S(1)}, u32[]{:S(2)}, u32[]{:S(2)}) collective-permute-start(f32[128,256]{1,0:T(8,128)S(1)} %get-tuple-element.35), channel_id=1, source_target_pairs={{0,2},{1,3},{2,0},{3,1},{4,6},{5,7},{6,4},{7,5},{8,10},{9,11},{10,... | collective-permute-start | bytes 393224 | tf_op jit(solution)/shard_map/ppermute | solution.py:20
  74.5 4.0 %collective-permute-start.7 = (f32[128,256]{1,0:T(8,128)S(1)}, f32[128,256]{1,0:T(8,128)S(1)}, u32[]{:S(2)}, u32[]{:S(2)}) collective-permute-start(f32[128,256]{1,0:T(8,128)S(1)} %get-tuple-element.37), channel_id=1, source_target_pairs={{0,2},{1,3},{2,0},{3,1},{4,6},{5,7},{6,4},{7,5},{8,10},{9,11},{10,... | collective-permute-start | bytes 393224 | tf_op jit(solution)/shard_map/ppermute | solution.py:20
  78.4 6.8 %collective-permute-done.4 = f32[128,256]{1,0:T(8,128)S(1)} collective-permute-done((f32[128,256]{1,0:T(8,128)S(1)}, f32[128,256]{1,0:T(8,128)S(1)}, u32[]{:S(2)}, u32[]{:S(2)}) %collective-permute-start.4) | collective-permute-done | bytes 131104 | tf_op jit(solution)/shard_map/ppermute | solution.py:20
  85.3 5.8 %collective-permute-start.6 = (f32[256,256]{1,0:T(8,128)S(1)}, f32[256,256]{1,0:T(8,128)S(1)}, u32[]{:S(2)}, u32[]{:S(2)}) collective-permute-start(f32[256,256]{1,0:T(8,128)S(1)} %bitcast.89), channel_id=1, source_target_pairs={{0,1},{1,0},{2,3},{3,2},{4,5},{5,4},{6,7},{7,6},{8,9},{9,8},{10,11... | collective-permute-start | bytes 786440 | tf_op jit(solution)/shard_map/ppermute | solution.py:20
  91.2 5.7 %collective-permute-done.6 = f32[256,256]{1,0:T(8,128)S(1)} collective-permute-done((f32[256,256]{1,0:T(8,128)S(1)}, f32[256,256]{1,0:T(8,128)S(1)}, u32[]{:S(2)}, u32[]{:S(2)}) %collective-permute-start.6) | collective-permute-done | bytes 262176 | tf_op jit(solution)/shard_map/ppermute | solution.py:20
  96.9 1.2 fusion.3
  98.0 3.3 %collective-permute-start.9 = (f32[512,1024]{1,0:T(8,128)S(1)}, f32[512,1024]{1,0:T(8,128)S(1)}, u32[]{:S(2)}, u32[]{:S(2)}) collective-permute-start(f32[512,1024]{1,0:T(8,128)S(1)} %fusion.3), channel_id=1, source_target_pairs={{0,64},{64,0},{1,65},{65,1},{2,66},{66,2},{3,67},{67,3},{4,68},{68... | collective-permute-start | bytes 6291464 | tf_op jit(solution)/shard_map/ppermute | solution.py:20
  101.4 3.4 %collective-permute-start.8 = (f32[256,256]{1,0:T(8,128)S(1)}, f32[256,256]{1,0:T(8,128)S(1)}, u32[]{:S(2)}, u32[]{:S(2)}) collective-permute-start(f32[256,256]{1,0:T(8,128)S(1)} %bitcast.87), channel_id=1, source_target_pairs={{0,1},{1,0},{2,3},{3,2},{4,5},{5,4},{6,7},{7,6},{8,9},{9,8},{10,11... | collective-permute-start | bytes 786440 | tf_op jit(solution)/shard_map/ppermute | solution.py:20
  104.8 3.6 %fusion.20 = f32[256,1024]{1,0:T(8,128)} fusion(f32[512,256]{1,0:T(8,128)S(1)} %bitcast.83, f32[512,1024]{1,0:T(8,128)} %bitcast.7), kind=kOutput, calls=%fused_computation.57 | convolution fusion | flops 805306368 | bytes 3670016 | tf_op jit(solution)/shard_map/dot_general | solution.py:38
  108.5 2.7 %collective-permute-done.8 = f32[256,256]{1,0:T(8,128)S(1)} collective-permute-done((f32[256,256]{1,0:T(8,128)S(1)}, f32[256,256]{1,0:T(8,128)S(1)}, u32[]{:S(2)}, u32[]{:S(2)}) %collective-permute-start.8) | collective-permute-done | bytes 262176 | tf_op jit(solution)/shard_map/ppermute | solution.py:20
  111.2 1.2 convolution_add_fusion
  112.4 30.7 %all_to_all.19 = f32[16,32,1024]{2,1,0:T(8,128)} all-to-all(f32[16,32,1024]{2,1,0:T(8,128)S(1)} %bitcast.79), channel_id=1, replica_groups=mesh['zh'=4,'core'=2,'y'=4,'x'=4,'t'=4] {'y','x'}, dimensions={0} | all-to-all | bytes 4194304 | tf_op jit(solution)/shard_map/all_to_all | solution.py:28
  143.0 1.7 reduce_sum.39
  144.8 13.1 %collective-permute-start.12 = (f32[16,1024]{1,0:T(8,128)S(1)}, f32[16,1024]{1,0:T(8,128)S(1)}, u32[]{:S(2)}, u32[]{:S(2)}) collective-permute-start(f32[16,1024]{1,0:T(8,128)S(1)} %get-tuple-element.26), channel_id=1, source_target_pairs={{0,384},{128,256},{256,128},{384,0},{1,385},{129,257},{257,129},{3... | collective-permute-start | bytes 196616 | tf_op jit(solution)/shard_map/ppermute | solution.py:20
  157.9 5.2 %collective-permute-start.10 = (f32[16,1024]{1,0:T(8,128)S(1)}, f32[16,1024]{1,0:T(8,128)S(1)}, u32[]{:S(2)}, u32[]{:S(2)}) collective-permute-start(f32[16,1024]{1,0:T(8,128)S(1)} %get-tuple-element.24), channel_id=1, source_target_pairs={{0,128},{128,0},{256,384},{384,256},{1,129},{129,1},{257,385},{385... | collective-permute-start | bytes 196616 | tf_op jit(solution)/shard_map/ppermute | solution.py:20
  163.1 3.9 %fusion = f32[256,1024]{1,0:T(8,128)} fusion(f32[256,1024]{1,0:T(8,128)} %fusion.20, f32[512,256]{1,0:T(8,128)S(1)} %bitcast.81, f32[512,1024]{1,0:T(8,128)} %collective-permute-done.1, f32[256,1024]{1,0:T(8,128)S(1)} %copy-done.1, f32[256]{0:T(256)S(1)} %convert_divide_fusion), kind=kOutput, calls=%fused_computation.2 | convolution fusion | flops 806354944 | bytes 5768192 | tf_op jit(solution)/shard_map/dot_general | solution.py:38
  167.1 5.3 %collective-permute-start.13 = (f32[16,1024]{1,0:T(8,128)S(1)}, f32[16,1024]{1,0:T(8,128)S(1)}, u32[]{:S(2)}, u32[]{:S(2)}) collective-permute-start(f32[16,1024]{1,0:T(8,128)S(1)} %add.166), channel_id=1, source_target_pairs={{0,128},{128,0},{256,384},{384,256},{1,129},{129,1},{257,385},{385... | collective-permute-start | bytes 196616 | tf_op jit(solution)/shard_map/ppermute | solution.py:20
  172.3 6.4 %collective-permute-start.11 = (f32[16,1024]{1,0:T(8,128)S(1)}, f32[16,1024]{1,0:T(8,128)S(1)}, u32[]{:S(2)}, u32[]{:S(2)}) collective-permute-start(f32[16,1024]{1,0:T(8,128)S(1)} %add.164), channel_id=1, source_target_pairs={{0,384},{128,256},{256,128},{384,0},{1,385},{129,257},{257,129},{3... | collective-permute-start | bytes 196616 | tf_op jit(solution)/shard_map/ppermute | solution.py:20
  178.8 3.3 %collective-permute-done.11 = f32[16,1024]{1,0:T(8,128)S(1)} collective-permute-done((f32[16,1024]{1,0:T(8,128)S(1)}, f32[16,1024]{1,0:T(8,128)S(1)}, u32[]{:S(2)}, u32[]{:S(2)}) %collective-permute-start.11) | collective-permute-done | bytes 65568 | tf_op jit(solution)/shard_map/ppermute | solution.py:20
  182.2 5.6 %collective-permute-start.14 = (f32[32,1024]{1,0:T(8,128)S(1)}, f32[32,1024]{1,0:T(8,128)S(1)}, u32[]{:S(2)}, u32[]{:S(2)}) collective-permute-start(f32[32,1024]{1,0:T(8,128)S(1)} %get-tuple-element.30), channel_id=1, source_target_pairs={{0,64},{64,0},{1,65},{65,1},{2,66},{66,2},{3,67},{67,3},{4,68},{68... | collective-permute-start | bytes 393224 | tf_op jit(solution)/shard_map/ppermute | solution.py:20
  (68 shorter events, 7.9 us)
Async XLA Ops:
  0.6 41.0 %copy-start = (s32[256,1024]{1,0:T(8,128)S(1)}, s32[256,1024]{1,0:T(8,128)}, u32[]{:S(2)}) copy-start(s32[256,1024]{1,0:T(8,128)} %param.8) | copy-start | bytes 3145732
  2.6 39.3 %copy-start.4 = (s32[1,16]{1,0:T(1,128)S(1)}, s32[1,16]{1,0:T(1,128)}, u32[]{:S(2)}) copy-start(s32[1,16]{1,0:T(1,128)} %param.9) | copy-start | bytes 196
  2.6 39.5 %copy-start.1 = (f32[256,1024]{1,0:T(8,128)S(1)}, f32[256,1024]{1,0:T(8,128)}, u32[]{:S(2)}) copy-start(f32[256,1024]{1,0:T(8,128)} %param.6) | copy-start | bytes 3145732
  36.2 14.8 %collective-permute-start.1 = (f32[512,1024]{1,0:T(8,128)}, f32[512,1024]{1,0:T(8,128)}, u32[]{:S(2)}, u32[]{:S(2)}) collective-permute-start(f32[512,1024]{1,0:T(8,128)} %bitcast.7), channel_id=1, source_target_pairs={{0,64},{64,0},{1,65},{65,1},{2,66},{66,2},{3,67},{67,3},{4,68},{68... | collective-permute-start | bytes 6291464 | tf_op jit(solution)/shard_map/ppermute | solution.py:20
  47.6 10.4 %collective-permute-start = (f32[2,136,256]{2,1,0:T(8,128)}, f32[2,136,256]{2,1,0:T(8,128)}, u32[]{:S(2)}, u32[]{:S(2)}) collective-permute-start(f32[2,136,256]{2,1,0:T(8,128)} %dynamic-slice_bitcast_fusion.1), channel_id=1, source_target_pairs={{0,1},{1,0},{2,3},{3,2},{4,5},{5,4},{6,7},{7,6},{8,9},{9,8},{10,11... | collective-permute-start | bytes 835592 | tf_op jit(solution)/shard_map/ppermute | solution.py:20
  55.4 16.1 %copy-start.3 = (s32[256]{0:T(256)S(1)}, s32[256]{0:T(256)}, u32[]{:S(2)}) copy-start(s32[256]{0:T(256)} %param.7) | copy-start | bytes 3076
  55.5 9.8 %collective-permute-start.3 = (f32[2,136,256]{2,1,0:T(8,128)S(1)}, f32[2,136,256]{2,1,0:T(8,128)S(1)}, u32[]{:S(2)}, u32[]{:S(2)}) collective-permute-start(f32[2,136,256]{2,1,0:T(8,128)S(1)} %dynamic-slice_bitcast_fusion), channel_id=1, source_target_pairs={{0,1},{1,0},{2,3},{3,2},{4,5},{5,4},{6,7},{7,6},{8,9},{9,8},{10,11... | collective-permute-start | bytes 835592 | tf_op jit(solution)/shard_map/ppermute | solution.py:20
  59.1 8.5 %collective-permute-start.2 = (f32[136,256]{1,0:T(8,128)S(1)}, f32[136,256]{1,0:T(8,128)S(1)}, u32[]{:S(2)}, u32[]{:S(2)}) collective-permute-start(f32[136,256]{1,0:T(8,128)S(1)} %dynamic-slice_bitcast_fusion.3), channel_id=1, source_target_pairs={{0,2},{1,3},{2,0},{3,1},{4,6},{5,7},{6,4},{7,5},{8,10},{9,11},{10,... | collective-permute-start | bytes 417800 | tf_op jit(solution)/shard_map/ppermute | solution.py:20
  67.6 6.7 %collective-permute-start.5 = (f32[136,256]{1,0:T(8,128)S(1)}, f32[136,256]{1,0:T(8,128)S(1)}, u32[]{:S(2)}, u32[]{:S(2)}) collective-permute-start(f32[136,256]{1,0:T(8,128)S(1)} %dynamic-slice_bitcast_fusion.2), channel_id=1, source_target_pairs={{0,2},{1,3},{2,0},{3,1},{4,6},{5,7},{6,4},{7,5},{8,10},{9,11},{10,... | collective-permute-start | bytes 417800 | tf_op jit(solution)/shard_map/ppermute | solution.py:20
  71.7 13.5 %collective-permute-start.4 = (f32[128,256]{1,0:T(8,128)S(1)}, f32[128,256]{1,0:T(8,128)S(1)}, u32[]{:S(2)}, u32[]{:S(2)}) collective-permute-start(f32[128,256]{1,0:T(8,128)S(1)} %get-tuple-element.35), channel_id=1, source_target_pairs={{0,2},{1,3},{2,0},{3,1},{4,6},{5,7},{6,4},{7,5},{8,10},{9,11},{10,... | collective-permute-start | bytes 393224 | tf_op jit(solution)/shard_map/ppermute | solution.py:20
  74.5 16.7 %collective-permute-start.7 = (f32[128,256]{1,0:T(8,128)S(1)}, f32[128,256]{1,0:T(8,128)S(1)}, u32[]{:S(2)}, u32[]{:S(2)}) collective-permute-start(f32[128,256]{1,0:T(8,128)S(1)} %get-tuple-element.37), channel_id=1, source_target_pairs={{0,2},{1,3},{2,0},{3,1},{4,6},{5,7},{6,4},{7,5},{8,10},{9,11},{10,... | collective-permute-start | bytes 393224 | tf_op jit(solution)/shard_map/ppermute | solution.py:20
  85.3 11.6 %collective-permute-start.6 = (f32[256,256]{1,0:T(8,128)S(1)}, f32[256,256]{1,0:T(8,128)S(1)}, u32[]{:S(2)}, u32[]{:S(2)}) collective-permute-start(f32[256,256]{1,0:T(8,128)S(1)} %bitcast.89), channel_id=1, source_target_pairs={{0,1},{1,0},{2,3},{3,2},{4,5},{5,4},{6,7},{7,6},{8,9},{9,8},{10,11... | collective-permute-start | bytes 786440 | tf_op jit(solution)/shard_map/ppermute | solution.py:20
  98.0 13.1 %collective-permute-start.9 = (f32[512,1024]{1,0:T(8,128)S(1)}, f32[512,1024]{1,0:T(8,128)S(1)}, u32[]{:S(2)}, u32[]{:S(2)}) collective-permute-start(f32[512,1024]{1,0:T(8,128)S(1)} %fusion.3), channel_id=1, source_target_pairs={{0,64},{64,0},{1,65},{65,1},{2,66},{66,2},{3,67},{67,3},{4,68},{68... | collective-permute-start | bytes 6291464 | tf_op jit(solution)/shard_map/ppermute | solution.py:20
  101.4 9.7 %collective-permute-start.8 = (f32[256,256]{1,0:T(8,128)S(1)}, f32[256,256]{1,0:T(8,128)S(1)}, u32[]{:S(2)}, u32[]{:S(2)}) collective-permute-start(f32[256,256]{1,0:T(8,128)S(1)} %bitcast.87), channel_id=1, source_target_pairs={{0,1},{1,0},{2,3},{3,2},{4,5},{5,4},{6,7},{7,6},{8,9},{9,8},{10,11... | collective-permute-start | bytes 786440 | tf_op jit(solution)/shard_map/ppermute | solution.py:20
  144.8 44.1 %copy-start.2 = (f32[64,1024]{1,0:T(8,128)S(1)}, f32[64,1024]{1,0:T(8,128)}, u32[]{:S(2)}) copy-start(f32[64,1024]{1,0:T(8,128)} %param.10) | copy-start | bytes 786436
  144.8 22.3 %collective-permute-start.12 = (f32[16,1024]{1,0:T(8,128)S(1)}, f32[16,1024]{1,0:T(8,128)S(1)}, u32[]{:S(2)}, u32[]{:S(2)}) collective-permute-start(f32[16,1024]{1,0:T(8,128)S(1)} %get-tuple-element.26), channel_id=1, source_target_pairs={{0,384},{128,256},{256,128},{384,0},{1,385},{129,257},{257,129},{3... | collective-permute-start | bytes 196616 | tf_op jit(solution)/shard_map/ppermute | solution.py:20
  157.9 9.1 %collective-permute-start.10 = (f32[16,1024]{1,0:T(8,128)S(1)}, f32[16,1024]{1,0:T(8,128)S(1)}, u32[]{:S(2)}, u32[]{:S(2)}) collective-permute-start(f32[16,1024]{1,0:T(8,128)S(1)} %get-tuple-element.24), channel_id=1, source_target_pairs={{0,128},{128,0},{256,384},{384,256},{1,129},{129,1},{257,385},{385... | collective-permute-start | bytes 196616 | tf_op jit(solution)/shard_map/ppermute | solution.py:20
  167.1 11.7 %collective-permute-start.13 = (f32[16,1024]{1,0:T(8,128)S(1)}, f32[16,1024]{1,0:T(8,128)S(1)}, u32[]{:S(2)}, u32[]{:S(2)}) collective-permute-start(f32[16,1024]{1,0:T(8,128)S(1)} %add.166), channel_id=1, source_target_pairs={{0,128},{128,0},{256,384},{384,256},{1,129},{129,1},{257,385},{385... | collective-permute-start | bytes 196616 | tf_op jit(solution)/shard_map/ppermute | solution.py:20
  172.3 9.8 %collective-permute-start.11 = (f32[16,1024]{1,0:T(8,128)S(1)}, f32[16,1024]{1,0:T(8,128)S(1)}, u32[]{:S(2)}, u32[]{:S(2)}) collective-permute-start(f32[16,1024]{1,0:T(8,128)S(1)} %add.164), channel_id=1, source_target_pairs={{0,384},{128,256},{256,128},{384,0},{1,385},{129,257},{257,129},{3... | collective-permute-start | bytes 196616 | tf_op jit(solution)/shard_map/ppermute | solution.py:20
  182.2 6.6 %collective-permute-start.14 = (f32[32,1024]{1,0:T(8,128)S(1)}, f32[32,1024]{1,0:T(8,128)S(1)}, u32[]{:S(2)}, u32[]{:S(2)}) collective-permute-start(f32[32,1024]{1,0:T(8,128)S(1)} %get-tuple-element.30), channel_id=1, source_target_pairs={{0,64},{64,0},{1,65},{65,1},{2,66},{66,2},{3,67},{67,3},{4,68},{68... | collective-permute-start | bytes 393224 | tf_op jit(solution)/shard_map/ppermute | solution.py:20

commit v3 on v2

--- a/solution.py
+++ b/solution.py
@@ -1,6 +1,8 @@
 import jax
 import jax.numpy as jnp
 from jax import lax
+from jax.experimental import pallas as pl
+from jax.experimental.pallas import tpu as pltpu
 from jax.sharding import Mesh, PartitionSpec as P
 
 
@@ -36,6 +38,50 @@
 
 def matmul(left, right, contract):
     return lax.dot_general(left, right, (contract, ((), ())), precision=lax.Precision.HIGH, preferred_element_type=jnp.float32)
+
+
+def high_and_low(value):
+    high = value.astype(jnp.bfloat16)
+    return high, (value - high.astype(jnp.float32)).astype(jnp.bfloat16)
+
+
+def parts_kernel(words_ref, mix_ref, mass_ref, parts_ref, mix_high, mix_low):
+    @pl.when(pl.program_id(0) == 0)
+    def _():
+        mix_high[...], mix_low[...] = high_and_low(mix_ref[...])
+
+    def product(left, right):
+        return lax.dot_general(left, right, (((1,), (1,)), ((), ())), preferred_element_type=jnp.float32)
+
+    chunk, topics = words_ref.shape
+    docs = mass_ref.shape[1]
+    words_high, words_low = high_and_low(words_ref[...])
+    small = product(words_high, mix_low[...]) + product(words_low, mix_high[...])
+    parts_ref[0, :chunk, :] = product(words_high, mix_high[...]) + small
+    ones = jnp.ones((EXTRA, topics), jnp.bfloat16)
+    word_sums = product(ones, words_high) + product(ones, words_low)
+    word_sums = jnp.concatenate([word_sums, jnp.zeros((EXTRA, docs - chunk), jnp.float32)], axis=1)
+    row = lax.broadcasted_iota(jnp.int32, (EXTRA, docs), 0)
+    parts_ref[0, chunk:, :] = jnp.where(row == 0, mass_ref[...], word_sums)
+
+
+def parts_of_words(words, mix, mass, chunks):
+    docs, topics = mix.shape
+    chunk = words.shape[0] // chunks
+    return pl.pallas_call(
+        parts_kernel,
+        out_shape=jax.ShapeDtypeStruct((chunks, chunk + EXTRA, docs), jnp.float32),
+        grid=(chunks,),
+        in_specs=[
+            pl.BlockSpec((chunk, topics), lambda i: (i, 0)),
+            pl.BlockSpec((docs, topics), lambda i: (0, 0)),
+            pl.BlockSpec((1, docs), lambda i: (0, 0)),
+        ],
+        out_specs=pl.BlockSpec((1, chunk + EXTRA, docs), lambda i: (i, 0, 0)),
+        scratch_shapes=[pltpu.VMEM((docs, topics), jnp.bfloat16), pltpu.VMEM((docs, topics), jnp.bfloat16)],
+        compiler_params=pltpu.CompilerParams(vmem_limit_bytes=16 * 2**20),
+        cost_estimate=pl.CostEstimate(flops=6 * chunks * chunk * docs * topics, bytes_accessed=4 * topics * (docs + chunks * chunk), transcendentals=0),
+    )(words, mix, mass)
 
 
 def first_partner(i):
@@ -85,10 +131,7 @@
         return lax.dynamic_index_in_dim(weights, wrapped(core + wave, CORES), 2, False).reshape(chunk, docs)
 
     def parts_of(wave, mix):
-        products = matmul(words[wave], mix, ((1,), (1,))).reshape(n_t, chunk, docs)
-        word_sums = jnp.sum(words[wave].reshape(n_cuts, half, topics), axis=2).reshape(n_t, 1, chunk)
-        word_sums = jnp.pad(word_sums, ((0, 0), (0, EXTRA - 2), (0, docs - chunk)))
-        parts = jnp.concatenate([products, jnp.broadcast_to(mass_part[None], (n_t, 1, docs)), word_sums], axis=1)
+        parts = parts_of_words(words[wave], mix, mass_part, n_t)
         return picked(parts.reshape(2, n_t // 2, chunk + EXTRA, docs), low)
 
     def picked(pair, place):

time: 190 us -> 187 us (0.984)
  starting transfers between devices: 74 us -> 63.8 us
  Pallas kernels: 0 us -> 9.31 us
  waiting for transfers between devices: 23.8 us -> 32.2 us
  matrix products: 15.1 us -> 9.9 us
  other arithmetic: 9.36 us -> 4.79 us
    ppermute x15, starting transfers between devices: 74 us -> 63.8 us  [moved(): lax.ppermute(block, axis, [(i, partner(i)) for i in range(lax.axis_size(a...]
    pallas_call x0 -> x2, Pallas kernels: none -> 9.31 us  [parts_of_words(): pl.pallas_call(parts_kernel, out_shape=jax.ShapeDtypeStruct((chunks, chun...]
    ppermute x15, waiting for transfers between devices: 23.8 us -> 32.2 us  [moved(): lax.ppermute(block, axis, [(i, partner(i)) for i in range(lax.axis_size(a...]
    dot_general x6 -> x4, matrix products: 15.1 us -> 9.9 us  [matmul(): lax.dot_general(left, right, (contract, ((), ())), precision=lax.Precisio...]
    reduce_sum x2 -> x0, other arithmetic: 3.53 us -> none  [parts_of(): jnp.sum(words[wave].reshape(n_cuts, half, topics), axis=2)]
  transfers between devices with their start and end apart: 15 -> 15, of which waited for: 9 -> 9; matrix products, arithmetic and copies ran while one was open for 10% -> 5% of each run, Pallas kernels for 0% -> 5%
where the time goes in v3:
time: 187 us
  blocking collectives  64.3 us (34%)
  starting transfers between devices  63.8 us (34%)
  waiting for transfers between devices  32.2 us (17%)
  matrix products  9.9 us (5%)
  Pallas kernels  9.31 us (5%)
  other arithmetic  4.79 us (3%)
    all_to_all x2, blocking collectives, exchanged(): return lax.all_to_all(blocks, axes, 0, 0, tiled=True)  64.3 us
    ppermute x15, starting transfers between devices, moved(): lax.ppermute(block, axis, [(i, partner(i)) for i in range(lax.axis_size(a...  63.8 us
    ppermute x15, waiting for transfers between devices, moved(): lax.ppermute(block, axis, [(i, partner(i)) for i in range(lax.axis_size(a...  32.2 us
    dot_general x4, matrix products, matmul(): lax.dot_general(left, right, (contract, ((), ())), precision=lax.Precisio...  9.9 us
    pallas_call x2, Pallas kernels, parts_of_words(): pl.pallas_call(parts_kernel, out_shape=jax.ShapeDtypeStruct((chunks, chun...  9.31 us
  transfers between devices with their start and end apart: 15, of which 9 were waited for; matrix products, arithmetic and copies ran while one was open for 5% of the time, Pallas kernels for 5%

profile of v3, /device:TPU:1, one launch (start us, length us, event | category | flops | bytes accessed | tf_op | source)
XLA Modules:
  0.0 186.5 jit_solution(732528231990761702)
XLA Ops:
  1.4 0.9 bitcast_divide_fusion
  2.6 33.6 %all_to_all.17 = f32[16,32,1024]{2,1,0:T(8,128)} all-to-all(f32[16,32,1024]{2,1,0:T(8,128)S(1)} %broadcast_in_dim.42), channel_id=1, replica_groups=mesh['zh'=4,'core'=2,'y'=4,'x'=4,'t'=4] {'y','x'}, dimensions={0} | all-to-all | bytes 4194304 | tf_op jit(solution)/shard_map/all_to_all | solution.py:30
  36.2 5.4 %collective-permute-start.1 = (f32[512,1024]{1,0:T(8,128)}, f32[512,1024]{1,0:T(8,128)}, u32[]{:S(2)}, u32[]{:S(2)}) collective-permute-start(f32[512,1024]{1,0:T(8,128)} %bitcast.2.words_ref), channel_id=1, source_target_pairs={{0,64},{64,0},{1,65},{65,1},{2,66},{66,2},{3,67},{67,3},{4,68},{68... | collective-permute-start | bytes 6291464 | tf_op jit(solution)/shard_map/ppermute | solution.py:22
  42.3 4.7 %shard_map.77 = f32[4,136,256]{2,1,0:T(8,128)S(1)} custom-call(f32[512,1024]{1,0:T(8,128)} %bitcast.2.words_ref, f32[256,1024]{1,0:T(8,128)S(1)} %copy-done.1, f32[1,256]{1,0:T(1,128)S(1)} %bitcast.75), custom_call_target="tpu_custom_call" | custom-call | flops 805306368 | bytes 3145728 | tf_op jit(solution)/shard_map/pallas_call | solution.py:71
  47.0 3.4 %collective-permute-start = (f32[2,136,256]{2,1,0:T(8,128)S(1)}, f32[2,136,256]{2,1,0:T(8,128)S(1)}, u32[]{:S(2)}, u32[]{:S(2)}) collective-permute-start(f32[2,136,256]{2,1,0:T(8,128)S(1)} %dynamic-slice_bitcast_fusion.1), channel_id=1, source_target_pairs={{0,1},{1,0},{2,3},{3,2},{4,5},{5,4},{6,7},{7,6},{8,9},{9,8},{10,11... | collective-permute-start | bytes 835592 | tf_op jit(solution)/shard_map/ppermute | solution.py:22
  50.5 4.7 %shard_map.78 = f32[4,136,256]{2,1,0:T(8,128)S(1)} custom-call(f32[512,1024]{1,0:T(8,128)} %collective-permute-done.1.words_ref, f32[256,1024]{1,0:T(8,128)S(1)} %copy-done.1, f32[1,256]{1,0:T(1,128)S(1)} %bitcast.76), custom_call_target="tpu_custom_call" | custom-call | flops 805306368 | bytes 3145728 | tf_op jit(solution)/shard_map/pallas_call | solution.py:71
  55.2 1.9 %collective-permute-start.3 = (f32[2,136,256]{2,1,0:T(8,128)S(1)}, f32[2,136,256]{2,1,0:T(8,128)S(1)}, u32[]{:S(2)}, u32[]{:S(2)}) collective-permute-start(f32[2,136,256]{2,1,0:T(8,128)S(1)} %dynamic-slice_bitcast_fusion), channel_id=1, source_target_pairs={{0,1},{1,0},{2,3},{3,2},{4,5},{5,4},{6,7},{7,6},{8,9},{9,8},{10,11... | collective-permute-start | bytes 835592 | tf_op jit(solution)/shard_map/ppermute | solution.py:22
  57.2 5.1 %collective-permute-start.2 = (f32[136,256]{1,0:T(8,128)S(1)}, f32[136,256]{1,0:T(8,128)S(1)}, u32[]{:S(2)}, u32[]{:S(2)}) collective-permute-start(f32[136,256]{1,0:T(8,128)S(1)} %dynamic-slice_bitcast_fusion.3), channel_id=1, source_target_pairs={{0,2},{1,3},{2,0},{3,1},{4,6},{5,7},{6,4},{7,5},{8,10},{9,11},{10,... | collective-permute-start | bytes 417800 | tf_op jit(solution)/shard_map/ppermute | solution.py:22
  62.3 5.7 %collective-permute-done.3 = f32[2,136,256]{2,1,0:T(8,128)S(1)} collective-permute-done((f32[2,136,256]{2,1,0:T(8,128)S(1)}, f32[2,136,256]{2,1,0:T(8,128)S(1)}, u32[]{:S(2)}, u32[]{:S(2)}) %collective-permute-start.3) | collective-permute-done | bytes 278560 | tf_op jit(solution)/shard_map/ppermute | solution.py:22
  68.1 2.8 %collective-permute-start.5 = (f32[136,256]{1,0:T(8,128)S(1)}, f32[136,256]{1,0:T(8,128)S(1)}, u32[]{:S(2)}, u32[]{:S(2)}) collective-permute-start(f32[136,256]{1,0:T(8,128)S(1)} %dynamic-slice_bitcast_fusion.2), channel_id=1, source_target_pairs={{0,2},{1,3},{2,0},{3,1},{4,6},{5,7},{6,4},{7,5},{8,10},{9,11},{10,... | collective-permute-start | bytes 417800 | tf_op jit(solution)/shard_map/ppermute | solution.py:22
  71.1 3.4 %collective-permute-start.4 = (f32[128,256]{1,0:T(8,128)S(1)}, f32[128,256]{1,0:T(8,128)S(1)}, u32[]{:S(2)}, u32[]{:S(2)}) collective-permute-start(f32[128,256]{1,0:T(8,128)S(1)} %get-tuple-element.35), channel_id=1, source_target_pairs={{0,2},{1,3},{2,0},{3,1},{4,6},{5,7},{6,4},{7,5},{8,10},{9,11},{10,... | collective-permute-start | bytes 393224 | tf_op jit(solution)/shard_map/ppermute | solution.py:22
  75.0 2.8 %collective-permute-start.7 = (f32[128,256]{1,0:T(8,128)S(1)}, f32[128,256]{1,0:T(8,128)S(1)}, u32[]{:S(2)}, u32[]{:S(2)}) collective-permute-start(f32[128,256]{1,0:T(8,128)S(1)} %get-tuple-element.37), channel_id=1, source_target_pairs={{0,2},{1,3},{2,0},{3,1},{4,6},{5,7},{6,4},{7,5},{8,10},{9,11},{10,... | collective-permute-start | bytes 393224 | tf_op jit(solution)/shard_map/ppermute | solution.py:22
  77.8 7.1 %collective-permute-done.4 = f32[128,256]{1,0:T(8,128)S(1)} collective-permute-done((f32[128,256]{1,0:T(8,128)S(1)}, f32[128,256]{1,0:T(8,128)S(1)}, u32[]{:S(2)}, u32[]{:S(2)}) %collective-permute-start.4) | collective-permute-done | bytes 131104 | tf_op jit(solution)/shard_map/ppermute | solution.py:22
  84.9 4.7 %collective-permute-start.6 = (f32[256,256]{1,0:T(8,128)S(1)}, f32[256,256]{1,0:T(8,128)S(1)}, u32[]{:S(2)}, u32[]{:S(2)}) collective-permute-start(f32[256,256]{1,0:T(8,128)S(1)} %bitcast.84), channel_id=1, source_target_pairs={{0,1},{1,0},{2,3},{3,2},{4,5},{5,4},{6,7},{7,6},{8,9},{9,8},{10,11... | collective-permute-start | bytes 786440 | tf_op jit(solution)/shard_map/ppermute | solution.py:22
  89.8 6.4 %collective-permute-done.6 = f32[256,256]{1,0:T(8,128)S(1)} collective-permute-done((f32[256,256]{1,0:T(8,128)S(1)}, f32[256,256]{1,0:T(8,128)S(1)}, u32[]{:S(2)}, u32[]{:S(2)}) %collective-permute-start.6) | collective-permute-done | bytes 262176 | tf_op jit(solution)/shard_map/ppermute | solution.py:22
  96.2 1.2 fusion.1
  97.3 3.3 %collective-permute-start.9 = (f32[512,1024]{1,0:T(8,128)S(1)}, f32[512,1024]{1,0:T(8,128)S(1)}, u32[]{:S(2)}, u32[]{:S(2)}) collective-permute-start(f32[512,1024]{1,0:T(8,128)S(1)} %fusion.1), channel_id=1, source_target_pairs={{0,64},{64,0},{1,65},{65,1},{2,66},{66,2},{3,67},{67,3},{4,68},{68... | collective-permute-start | bytes 6291464 | tf_op jit(solution)/shard_map/ppermute | solution.py:22
  100.7 2.7 %collective-permute-start.8 = (f32[256,256]{1,0:T(8,128)S(1)}, f32[256,256]{1,0:T(8,128)S(1)}, u32[]{:S(2)}, u32[]{:S(2)}) collective-permute-start(f32[256,256]{1,0:T(8,128)S(1)} %bitcast.82), channel_id=1, source_target_pairs={{0,1},{1,0},{2,3},{3,2},{4,5},{5,4},{6,7},{7,6},{8,9},{9,8},{10,11... | collective-permute-start | bytes 786440 | tf_op jit(solution)/shard_map/ppermute | solution.py:22
  103.4 3.6 %fusion.17 = f32[256,1024]{1,0:T(8,128)} fusion(f32[512,256]{1,0:T(8,128)S(1)} %bitcast.81, f32[512,1024]{1,0:T(8,128)} %bitcast.2.words_ref), kind=kOutput, calls=%fused_computation.51 | convolution fusion | flops 805306368 | bytes 3670016 | tf_op jit(solution)/shard_map/dot_general | solution.py:40
  107.1 3.3 %collective-permute-done.8 = f32[256,256]{1,0:T(8,128)S(1)} collective-permute-done((f32[256,256]{1,0:T(8,128)S(1)}, f32[256,256]{1,0:T(8,128)S(1)}, u32[]{:S(2)}, u32[]{:S(2)}) %collective-permute-start.8) | collective-permute-done | bytes 262176 | tf_op jit(solution)/shard_map/ppermute | solution.py:22
  110.4 1.2 convolution_add_fusion
  111.6 30.7 %all_to_all.18 = f32[16,32,1024]{2,1,0:T(8,128)} all-to-all(f32[16,32,1024]{2,1,0:T(8,128)S(1)} %bitcast.77), channel_id=1, replica_groups=mesh['zh'=4,'core'=2,'y'=4,'x'=4,'t'=4] {'y','x'}, dimensions={0} | all-to-all | bytes 4194304 | tf_op jit(solution)/shard_map/all_to_all | solution.py:30
  142.3 1.7 reduce_sum.19
  144.1 10.8 %collective-permute-start.12 = (f32[16,1024]{1,0:T(8,128)S(1)}, f32[16,1024]{1,0:T(8,128)S(1)}, u32[]{:S(2)}, u32[]{:S(2)}) collective-permute-start(f32[16,1024]{1,0:T(8,128)S(1)} %get-tuple-element.26), channel_id=1, source_target_pairs={{0,384},{128,256},{256,128},{384,0},{1,385},{129,257},{257,129},{3... | collective-permute-start | bytes 196616 | tf_op jit(solution)/shard_map/ppermute | solution.py:22
  154.9 5.2 %collective-permute-start.10 = (f32[16,1024]{1,0:T(8,128)S(1)}, f32[16,1024]{1,0:T(8,128)S(1)}, u32[]{:S(2)}, u32[]{:S(2)}) collective-permute-start(f32[16,1024]{1,0:T(8,128)S(1)} %get-tuple-element.24), channel_id=1, source_target_pairs={{0,128},{128,0},{256,384},{384,256},{1,129},{129,1},{257,385},{385... | collective-permute-start | bytes 196616 | tf_op jit(solution)/shard_map/ppermute | solution.py:22
  160.0 3.9 %fusion = f32[256,1024]{1,0:T(8,128)} fusion(f32[256,1024]{1,0:T(8,128)} %fusion.17, f32[512,256]{1,0:T(8,128)S(1)} %bitcast.79, f32[512,1024]{1,0:T(8,128)} %collective-permute-done.1.words_ref, f32[256,1024]{1,0:T(8,128)S(1)} %copy-done.1, f32[256]{0:T(256)S(1)} %convert_divide_fusion), kind=kOutput, calls=%fused_computation.2 | convolution fusion | flops 806354944 | bytes 5768192 | tf_op jit(solution)/shard_map/dot_general | solution.py:40
  164.9 4.4 %collective-permute-start.13 = (f32[16,1024]{1,0:T(8,128)S(1)}, f32[16,1024]{1,0:T(8,128)S(1)}, u32[]{:S(2)}, u32[]{:S(2)}) collective-permute-start(f32[16,1024]{1,0:T(8,128)S(1)} %add.162), channel_id=1, source_target_pairs={{0,128},{128,0},{256,384},{384,256},{1,129},{129,1},{257,385},{385... | collective-permute-start | bytes 196616 | tf_op jit(solution)/shard_map/ppermute | solution.py:22
  169.3 2.6 %collective-permute-start.11 = (f32[16,1024]{1,0:T(8,128)S(1)}, f32[16,1024]{1,0:T(8,128)S(1)}, u32[]{:S(2)}, u32[]{:S(2)}) collective-permute-start(f32[16,1024]{1,0:T(8,128)S(1)} %add.160), channel_id=1, source_target_pairs={{0,384},{128,256},{256,128},{384,0},{1,385},{129,257},{257,129},{3... | collective-permute-start | bytes 196616 | tf_op jit(solution)/shard_map/ppermute | solution.py:22
  171.9 2.6 %collective-permute-done.13 = f32[16,1024]{1,0:T(8,128)S(1)} collective-permute-done((f32[16,1024]{1,0:T(8,128)S(1)}, f32[16,1024]{1,0:T(8,128)S(1)}, u32[]{:S(2)}, u32[]{:S(2)}) %collective-permute-start.13) | collective-permute-done | bytes 65568 | tf_op jit(solution)/shard_map/ppermute | solution.py:22
  174.5 4.8 %collective-permute-done.11 = f32[16,1024]{1,0:T(8,128)S(1)} collective-permute-done((f32[16,1024]{1,0:T(8,128)S(1)}, f32[16,1024]{1,0:T(8,128)S(1)}, u32[]{:S(2)}, u32[]{:S(2)}) %collective-permute-start.11) | collective-permute-done | bytes 65568 | tf_op jit(solution)/shard_map/ppermute | solution.py:22
  179.4 5.4 %collective-permute-start.14 = (f32[32,1024]{1,0:T(8,128)S(1)}, f32[32,1024]{1,0:T(8,128)S(1)}, u32[]{:S(2)}, u32[]{:S(2)}) collective-permute-start(f32[32,1024]{1,0:T(8,128)S(1)} %get-tuple-element.30), channel_id=1, source_target_pairs={{0,64},{64,0},{1,65},{65,1},{2,66},{66,2},{3,67},{67,3},{4,68},{68... | collective-permute-start | bytes 393224 | tf_op jit(solution)/shard_map/ppermute | solution.py:22
  184.8 1.0 collective-permute-done.14
  (60 shorter events, 4.5 us)
Async XLA Ops:
  0.6 41.0 %copy-start = (s32[256,1024]{1,0:T(8,128)S(1)}, s32[256,1024]{1,0:T(8,128)}, u32[]{:S(2)}) copy-start(s32[256,1024]{1,0:T(8,128)} %param.8) | copy-start | bytes 3145732
  2.6 39.3 %copy-start.4 = (s32[1,16]{1,0:T(1,128)S(1)}, s32[1,16]{1,0:T(1,128)}, u32[]{:S(2)}) copy-start(s32[1,16]{1,0:T(1,128)} %param.9) | copy-start | bytes 196
  2.6 39.5 %copy-start.1 = (f32[256,1024]{1,0:T(8,128)S(1)}, f32[256,1024]{1,0:T(8,128)}, u32[]{:S(2)}) copy-start(f32[256,1024]{1,0:T(8,128)} %mix_ref.2) | copy-start | bytes 3145732
  36.2 14.2 %collective-permute-start.1 = (f32[512,1024]{1,0:T(8,128)}, f32[512,1024]{1,0:T(8,128)}, u32[]{:S(2)}, u32[]{:S(2)}) collective-permute-start(f32[512,1024]{1,0:T(8,128)} %bitcast.2.words_ref), channel_id=1, source_target_pairs={{0,64},{64,0},{1,65},{65,1},{2,66},{66,2},{3,67},{67,3},{4,68},{68... | collective-permute-start | bytes 6291464 | tf_op jit(solution)/shard_map/ppermute | solution.py:22
  47.0 10.1 %collective-permute-start = (f32[2,136,256]{2,1,0:T(8,128)S(1)}, f32[2,136,256]{2,1,0:T(8,128)S(1)}, u32[]{:S(2)}, u32[]{:S(2)}) collective-permute-start(f32[2,136,256]{2,1,0:T(8,128)S(1)} %dynamic-slice_bitcast_fusion.1), channel_id=1, source_target_pairs={{0,1},{1,0},{2,3},{3,2},{4,5},{5,4},{6,7},{7,6},{8,9},{9,8},{10,11... | collective-permute-start | bytes 835592 | tf_op jit(solution)/shard_map/ppermute | solution.py:22
  55.1 15.8 %copy-start.3 = (s32[256]{0:T(256)S(1)}, s32[256]{0:T(256)}, u32[]{:S(2)}) copy-start(s32[256]{0:T(256)} %param.7) | copy-start | bytes 3076
  55.2 12.8 %collective-permute-start.3 = (f32[2,136,256]{2,1,0:T(8,128)S(1)}, f32[2,136,256]{2,1,0:T(8,128)S(1)}, u32[]{:S(2)}, u32[]{:S(2)}) collective-permute-start(f32[2,136,256]{2,1,0:T(8,128)S(1)} %dynamic-slice_bitcast_fusion), channel_id=1, source_target_pairs={{0,1},{1,0},{2,3},{3,2},{4,5},{5,4},{6,7},{7,6},{8,9},{9,8},{10,11... | collective-permute-start | bytes 835592 | tf_op jit(solution)/shard_map/ppermute | solution.py:22
  57.2 10.8 %collective-permute-start.2 = (f32[136,256]{1,0:T(8,128)S(1)}, f32[136,256]{1,0:T(8,128)S(1)}, u32[]{:S(2)}, u32[]{:S(2)}) collective-permute-start(f32[136,256]{1,0:T(8,128)S(1)} %dynamic-slice_bitcast_fusion.3), channel_id=1, source_target_pairs={{0,2},{1,3},{2,0},{3,1},{4,6},{5,7},{6,4},{7,5},{8,10},{9,11},{10,... | collective-permute-start | bytes 417800 | tf_op jit(solution)/shard_map/ppermute | solution.py:22
  68.1 6.7 %collective-permute-start.5 = (f32[136,256]{1,0:T(8,128)S(1)}, f32[136,256]{1,0:T(8,128)S(1)}, u32[]{:S(2)}, u32[]{:S(2)}) collective-permute-start(f32[136,256]{1,0:T(8,128)S(1)} %dynamic-slice_bitcast_fusion.2), channel_id=1, source_target_pairs={{0,2},{1,3},{2,0},{3,1},{4,6},{5,7},{6,4},{7,5},{8,10},{9,11},{10,... | collective-permute-start | bytes 417800 | tf_op jit(solution)/shard_map/ppermute | solution.py:22
  71.1 13.9 %collective-permute-start.4 = (f32[128,256]{1,0:T(8,128)S(1)}, f32[128,256]{1,0:T(8,128)S(1)}, u32[]{:S(2)}, u32[]{:S(2)}) collective-permute-start(f32[128,256]{1,0:T(8,128)S(1)} %get-tuple-element.35), channel_id=1, source_target_pairs={{0,2},{1,3},{2,0},{3,1},{4,6},{5,7},{6,4},{7,5},{8,10},{9,11},{10,... | collective-permute-start | bytes 393224 | tf_op jit(solution)/shard_map/ppermute | solution.py:22
  75.0 14.8 %collective-permute-start.7 = (f32[128,256]{1,0:T(8,128)S(1)}, f32[128,256]{1,0:T(8,128)S(1)}, u32[]{:S(2)}, u32[]{:S(2)}) collective-permute-start(f32[128,256]{1,0:T(8,128)S(1)} %get-tuple-element.37), channel_id=1, source_target_pairs={{0,2},{1,3},{2,0},{3,1},{4,6},{5,7},{6,4},{7,5},{8,10},{9,11},{10,... | collective-permute-start | bytes 393224 | tf_op jit(solution)/shard_map/ppermute | solution.py:22
  84.9 11.2 %collective-permute-start.6 = (f32[256,256]{1,0:T(8,128)S(1)}, f32[256,256]{1,0:T(8,128)S(1)}, u32[]{:S(2)}, u32[]{:S(2)}) collective-permute-start(f32[256,256]{1,0:T(8,128)S(1)} %bitcast.84), channel_id=1, source_target_pairs={{0,1},{1,0},{2,3},{3,2},{4,5},{5,4},{6,7},{7,6},{8,9},{9,8},{10,11... | collective-permute-start | bytes 786440 | tf_op jit(solution)/shard_map/ppermute | solution.py:22
  97.3 13.1 %collective-permute-start.9 = (f32[512,1024]{1,0:T(8,128)S(1)}, f32[512,1024]{1,0:T(8,128)S(1)}, u32[]{:S(2)}, u32[]{:S(2)}) collective-permute-start(f32[512,1024]{1,0:T(8,128)S(1)} %fusion.1), channel_id=1, source_target_pairs={{0,64},{64,0},{1,65},{65,1},{2,66},{66,2},{3,67},{67,3},{4,68},{68... | collective-permute-start | bytes 6291464 | tf_op jit(solution)/shard_map/ppermute | solution.py:22
  100.7 9.7 %collective-permute-start.8 = (f32[256,256]{1,0:T(8,128)S(1)}, f32[256,256]{1,0:T(8,128)S(1)}, u32[]{:S(2)}, u32[]{:S(2)}) collective-permute-start(f32[256,256]{1,0:T(8,128)S(1)} %bitcast.82), channel_id=1, source_target_pairs={{0,1},{1,0},{2,3},{3,2},{4,5},{5,4},{6,7},{7,6},{8,9},{9,8},{10,11... | collective-permute-start | bytes 786440 | tf_op jit(solution)/shard_map/ppermute | solution.py:22
  144.0 41.7 %copy-start.2 = (f32[64,1024]{1,0:T(8,128)S(1)}, f32[64,1024]{1,0:T(8,128)}, u32[]{:S(2)}) copy-start(f32[64,1024]{1,0:T(8,128)} %param.10) | copy-start | bytes 786436
  144.1 20.8 %collective-permute-start.12 = (f32[16,1024]{1,0:T(8,128)S(1)}, f32[16,1024]{1,0:T(8,128)S(1)}, u32[]{:S(2)}, u32[]{:S(2)}) collective-permute-start(f32[16,1024]{1,0:T(8,128)S(1)} %get-tuple-element.26), channel_id=1, source_target_pairs={{0,384},{128,256},{256,128},{384,0},{1,385},{129,257},{257,129},{3... | collective-permute-start | bytes 196616 | tf_op jit(solution)/shard_map/ppermute | solution.py:22
  154.9 10.0 %collective-permute-start.10 = (f32[16,1024]{1,0:T(8,128)S(1)}, f32[16,1024]{1,0:T(8,128)S(1)}, u32[]{:S(2)}, u32[]{:S(2)}) collective-permute-start(f32[16,1024]{1,0:T(8,128)S(1)} %get-tuple-element.24), channel_id=1, source_target_pairs={{0,128},{128,0},{256,384},{384,256},{1,129},{129,1},{257,385},{385... | collective-permute-start | bytes 196616 | tf_op jit(solution)/shard_map/ppermute | solution.py:22
  164.9 9.6 %collective-permute-start.13 = (f32[16,1024]{1,0:T(8,128)S(1)}, f32[16,1024]{1,0:T(8,128)S(1)}, u32[]{:S(2)}, u32[]{:S(2)}) collective-permute-start(f32[16,1024]{1,0:T(8,128)S(1)} %add.162), channel_id=1, source_target_pairs={{0,128},{128,0},{256,384},{384,256},{1,129},{129,1},{257,385},{385... | collective-permute-start | bytes 196616 | tf_op jit(solution)/shard_map/ppermute | solution.py:22
  169.3 10.0 %collective-permute-start.11 = (f32[16,1024]{1,0:T(8,128)S(1)}, f32[16,1024]{1,0:T(8,128)S(1)}, u32[]{:S(2)}, u32[]{:S(2)}) collective-permute-start(f32[16,1024]{1,0:T(8,128)S(1)} %add.160), channel_id=1, source_target_pairs={{0,384},{128,256},{256,128},{384,0},{1,385},{129,257},{257,129},{3... | collective-permute-start | bytes 196616 | tf_op jit(solution)/shard_map/ppermute | solution.py:22
  179.4 6.4 %collective-permute-start.14 = (f32[32,1024]{1,0:T(8,128)S(1)}, f32[32,1024]{1,0:T(8,128)S(1)}, u32[]{:S(2)}, u32[]{:S(2)}) collective-permute-start(f32[32,1024]{1,0:T(8,128)S(1)} %get-tuple-element.30), channel_id=1, source_target_pairs={{0,64},{64,0},{1,65},{65,1},{2,66},{66,2},{3,67},{67,3},{4,68},{68... | collective-permute-start | bytes 393224 | tf_op jit(solution)/shard_map/ppermute | solution.py:22

commit v4 on v3

--- a/solution.py
+++ b/solution.py
@@ -12,6 +12,7 @@
 
 CORES = 2
 EXTRA = 8
+STEPS = 2
 
 
 def wrapped(place, size):
@@ -45,24 +46,31 @@
     return high, (value - high.astype(jnp.float32)).astype(jnp.bfloat16)
 
 
-def parts_kernel(words_ref, mix_ref, mass_ref, parts_ref, mix_high, mix_low):
-    @pl.when(pl.program_id(0) == 0)
-    def _():
-        mix_high[...], mix_low[...] = high_and_low(mix_ref[...])
-
+def parts_kernel(words_ref, mix_ref, mass_ref, parts_ref):
     def product(left, right):
         return lax.dot_general(left, right, (((1,), (1,)), ((), ())), preferred_element_type=jnp.float32)
 
-    chunk, topics = words_ref.shape
-    docs = mass_ref.shape[1]
+    chunks, rows, docs = parts_ref.shape
+    chunk = rows - EXTRA
+    first = pl.program_id(0) == 0
+
+    @pl.when(first)
+    def _():
+        parts_ref[...] = jnp.zeros_like(parts_ref)
+
+    mix_high, mix_low = high_and_low(mix_ref[...])
     words_high, words_low = high_and_low(words_ref[...])
-    small = product(words_high, mix_low[...]) + product(words_low, mix_high[...])
-    parts_ref[0, :chunk, :] = product(words_high, mix_high[...]) + small
-    ones = jnp.ones((EXTRA, topics), jnp.bfloat16)
-    word_sums = product(ones, words_high) + product(ones, words_low)
-    word_sums = jnp.concatenate([word_sums, jnp.zeros((EXTRA, docs - chunk), jnp.float32)], axis=1)
+    products = product(words_high, mix_low) + product(words_low, mix_high) + product(words_high, mix_high)
+    diagonal = lax.broadcasted_iota(jnp.int32, (chunk, chunk), 0) == lax.broadcasted_iota(jnp.int32, (chunk, chunk), 1)
     row = lax.broadcasted_iota(jnp.int32, (EXTRA, docs), 0)
-    parts_ref[0, chunk:, :] = jnp.where(row == 0, mass_ref[...], word_sums)
+    mass = jnp.where(first, mass_ref[...], 0.0)
+    for c in range(chunks):
+        span = slice(c * chunk, (c + 1) * chunk)
+        sums = jnp.sum(words_ref[span, :], axis=1, keepdims=True)
+        sums = jnp.sum(jnp.where(diagonal, sums, 0.0), axis=0, keepdims=True)
+        sums = jnp.concatenate([sums, jnp.zeros((1, docs - chunk), jnp.float32)], axis=1)
+        parts_ref[c, :chunk, :] += products[span]
+        parts_ref[c, chunk:, :] += jnp.where(row == 0, mass, sums)
 
 
 def parts_of_words(words, mix, mass, chunks):
@@ -71,15 +79,14 @@
     return pl.pallas_call(
         parts_kernel,
         out_shape=jax.ShapeDtypeStruct((chunks, chunk + EXTRA, docs), jnp.float32),
-        grid=(chunks,),
+        grid=(STEPS,),
         in_specs=[
-            pl.BlockSpec((chunk, topics), lambda i: (i, 0)),
-            pl.BlockSpec((docs, topics), lambda i: (0, 0)),
+            pl.BlockSpec((chunks * chunk, topics // STEPS), lambda i: (0, i)),
+            pl.BlockSpec((docs, topics // STEPS), lambda i: (0, i)),
             pl.BlockSpec((1, docs), lambda i: (0, 0)),
         ],
-        out_specs=pl.BlockSpec((1, chunk + EXTRA, docs), lambda i: (i, 0, 0)),
-        scratch_shapes=[pltpu.VMEM((docs, topics), jnp.bfloat16), pltpu.VMEM((docs, topics), jnp.bfloat16)],
-        compiler_params=pltpu.CompilerParams(vmem_limit_bytes=16 * 2**20),
+        out_specs=pl.BlockSpec((chunks, chunk + EXTRA, docs), lambda i: (0, 0, 0)),
+        compiler_params=pltpu.CompilerParams(vmem_limit_bytes=24 * 2**20),
         cost_estimate=pl.CostEstimate(flops=6 * chunks * chunk * docs * topics, bytes_accessed=4 * topics * (docs + chunks * chunk), transcendentals=0),
     )(words, mix, mass)
 

time: 187 us -> 184 us (0.984)
  Pallas kernels: 9.31 us -> 5.1 us
  starting transfers between devices: 63.8 us -> 66.3 us
    pallas_call x2, Pallas kernels: 9.31 us -> 5.1 us  [parts_of_words(): pl.pallas_call(parts_kernel, out_shape=jax.ShapeDtypeStruct((chunks, chun...]
    ppermute x15, starting transfers between devices: 63.8 us -> 66.3 us  [moved(): lax.ppermute(block, axis, [(i, partner(i)) for i in range(lax.axis_size(a...]
  transfers between devices with their start and end apart: 15 -> 15, of which waited for: 9 -> 9; matrix products, arithmetic and copies ran while one was open for 5% -> 5% of each run, Pallas kernels for 5% -> 3%
where the time goes in v4:
time: 184 us; the launch traced here: 183 us
  starting transfers between devices  66.3 us (36%)
  blocking collectives  64.3 us (35%)
  waiting for transfers between devices  30.9 us (17%)
  matrix products  9.9 us (5%)
  Pallas kernels  5.1 us (3%)
  other arithmetic  4.79 us (3%)
    ppermute x15, starting transfers between devices, moved(): lax.ppermute(block, axis, [(i, partner(i)) for i in range(lax.axis_size(a...  66.3 us
    all_to_all x2, blocking collectives, exchanged(): return lax.all_to_all(blocks, axes, 0, 0, tiled=True)  64.3 us
    ppermute x15, waiting for transfers between devices, moved(): lax.ppermute(block, axis, [(i, partner(i)) for i in range(lax.axis_size(a...  30.9 us
    dot_general x4, matrix products, matmul(): lax.dot_general(left, right, (contract, ((), ())), precision=lax.Precisio...  9.9 us
    pallas_call x2, Pallas kernels, parts_of_words(): pl.pallas_call(parts_kernel, out_shape=jax.ShapeDtypeStruct((chunks, chun...  5.1 us
  transfers between devices with their start and end apart: 15, of which 9 were waited for; matrix products, arithmetic and copies ran while one was open for 5% of the time, Pallas kernels for 3%

profile of v4, /device:TPU:1, one launch (start us, length us, event | category | flops | bytes accessed | tf_op | source)
XLA Modules:
  0.0 183.5 jit_solution(2149390623430696598)
XLA Ops:
  1.4 0.9 bitcast_divide_fusion
  2.6 33.6 %all_to_all.17 = f32[16,32,1024]{2,1,0:T(8,128)} all-to-all(f32[16,32,1024]{2,1,0:T(8,128)S(1)} %broadcast_in_dim.42), channel_id=1, replica_groups=mesh['zh'=4,'core'=2,'y'=4,'x'=4,'t'=4] {'y','x'}, dimensions={0} | all-to-all | bytes 4194304 | tf_op jit(solution)/shard_map/all_to_all | solution.py:31
  36.2 5.4 %collective-permute-start.1 = (f32[512,1024]{1,0:T(8,128)}, f32[512,1024]{1,0:T(8,128)}, u32[]{:S(2)}, u32[]{:S(2)}) collective-permute-start(f32[512,1024]{1,0:T(8,128)} %bitcast.2.words_ref), channel_id=1, source_target_pairs={{0,64},{64,0},{1,65},{65,1},{2,66},{66,2},{3,67},{67,3},{4,68},{68... | collective-permute-start | bytes 6291464 | tf_op jit(solution)/shard_map/ppermute | solution.py:23
  42.3 2.6 %shard_map.77 = f32[4,136,256]{2,1,0:T(8,128)S(1)} custom-call(f32[512,1024]{1,0:T(8,128)} %bitcast.2.words_ref, f32[256,1024]{1,0:T(8,128)S(1)} %copy-done.1, f32[1,256]{1,0:T(1,128)S(1)} %bitcast.75), custom_call_target="tpu_custom_call" | custom-call | flops 805306368 | bytes 3145728 | tf_op jit(solution)/shard_map/pallas_call | solution.py:79
  44.9 3.4 %collective-permute-start = (f32[2,136,256]{2,1,0:T(8,128)S(1)}, f32[2,136,256]{2,1,0:T(8,128)S(1)}, u32[]{:S(2)}, u32[]{:S(2)}) collective-permute-start(f32[2,136,256]{2,1,0:T(8,128)S(1)} %dynamic-slice_bitcast_fusion.1), channel_id=1, source_target_pairs={{0,1},{1,0},{2,3},{3,2},{4,5},{5,4},{6,7},{7,6},{8,9},{9,8},{10,11... | collective-permute-start | bytes 835592 | tf_op jit(solution)/shard_map/ppermute | solution.py:23
  48.4 2.6 %shard_map.78 = f32[4,136,256]{2,1,0:T(8,128)S(1)} custom-call(f32[512,1024]{1,0:T(8,128)} %collective-permute-done.1.words_ref, f32[256,1024]{1,0:T(8,128)S(1)} %copy-done.1, f32[1,256]{1,0:T(1,128)S(1)} %bitcast.76), custom_call_target="tpu_custom_call" | custom-call | flops 805306368 | bytes 3145728 | tf_op jit(solution)/shard_map/pallas_call | solution.py:79
  51.0 1.9 %collective-permute-start.3 = (f32[2,136,256]{2,1,0:T(8,128)S(1)}, f32[2,136,256]{2,1,0:T(8,128)S(1)}, u32[]{:S(2)}, u32[]{:S(2)}) collective-permute-start(f32[2,136,256]{2,1,0:T(8,128)S(1)} %dynamic-slice_bitcast_fusion), channel_id=1, source_target_pairs={{0,1},{1,0},{2,3},{3,2},{4,5},{5,4},{6,7},{7,6},{8,9},{9,8},{10,11... | collective-permute-start | bytes 835592 | tf_op jit(solution)/shard_map/ppermute | solution.py:23
  52.9 2.2 %collective-permute-done = f32[2,136,256]{2,1,0:T(8,128)S(1)} collective-permute-done((f32[2,136,256]{2,1,0:T(8,128)S(1)}, f32[2,136,256]{2,1,0:T(8,128)S(1)}, u32[]{:S(2)}, u32[]{:S(2)}) %collective-permute-start) | collective-permute-done | bytes 278560 | tf_op jit(solution)/shard_map/ppermute | solution.py:23
  55.1 5.1 %collective-permute-start.2 = (f32[136,256]{1,0:T(8,128)S(1)}, f32[136,256]{1,0:T(8,128)S(1)}, u32[]{:S(2)}, u32[]{:S(2)}) collective-permute-start(f32[136,256]{1,0:T(8,128)S(1)} %dynamic-slice_bitcast_fusion.3), channel_id=1, source_target_pairs={{0,2},{1,3},{2,0},{3,1},{4,6},{5,7},{6,4},{7,5},{8,10},{9,11},{10,... | collective-permute-start | bytes 417800 | tf_op jit(solution)/shard_map/ppermute | solution.py:23
  60.8 2.9 %collective-permute-done.2 = f32[136,256]{1,0:T(8,128)S(1)} collective-permute-done((f32[136,256]{1,0:T(8,128)S(1)}, f32[136,256]{1,0:T(8,128)S(1)}, u32[]{:S(2)}, u32[]{:S(2)}) %collective-permute-start.2) | collective-permute-done | bytes 139296 | tf_op jit(solution)/shard_map/ppermute | solution.py:23
  63.7 4.0 %collective-permute-start.5 = (f32[136,256]{1,0:T(8,128)S(1)}, f32[136,256]{1,0:T(8,128)S(1)}, u32[]{:S(2)}, u32[]{:S(2)}) collective-permute-start(f32[136,256]{1,0:T(8,128)S(1)} %dynamic-slice_bitcast_fusion.2), channel_id=1, source_target_pairs={{0,2},{1,3},{2,0},{3,1},{4,6},{5,7},{6,4},{7,5},{8,10},{9,11},{10,... | collective-permute-start | bytes 417800 | tf_op jit(solution)/shard_map/ppermute | solution.py:23
  67.9 2.1 %collective-permute-start.4 = (f32[128,256]{1,0:T(8,128)S(1)}, f32[128,256]{1,0:T(8,128)S(1)}, u32[]{:S(2)}, u32[]{:S(2)}) collective-permute-start(f32[128,256]{1,0:T(8,128)S(1)} %get-tuple-element.35), channel_id=1, source_target_pairs={{0,2},{1,3},{2,0},{3,1},{4,6},{5,7},{6,4},{7,5},{8,10},{9,11},{10,... | collective-permute-start | bytes 393224 | tf_op jit(solution)/shard_map/ppermute | solution.py:23
  70.6 4.0 %collective-permute-start.7 = (f32[128,256]{1,0:T(8,128)S(1)}, f32[128,256]{1,0:T(8,128)S(1)}, u32[]{:S(2)}, u32[]{:S(2)}) collective-permute-start(f32[128,256]{1,0:T(8,128)S(1)} %get-tuple-element.37), channel_id=1, source_target_pairs={{0,2},{1,3},{2,0},{3,1},{4,6},{5,7},{6,4},{7,5},{8,10},{9,11},{10,... | collective-permute-start | bytes 393224 | tf_op jit(solution)/shard_map/ppermute | solution.py:23
  74.6 7.0 %collective-permute-done.4 = f32[128,256]{1,0:T(8,128)S(1)} collective-permute-done((f32[128,256]{1,0:T(8,128)S(1)}, f32[128,256]{1,0:T(8,128)S(1)}, u32[]{:S(2)}, u32[]{:S(2)}) %collective-permute-start.4) | collective-permute-done | bytes 131104 | tf_op jit(solution)/shard_map/ppermute | solution.py:23
  81.7 5.7 %collective-permute-start.6 = (f32[256,256]{1,0:T(8,128)S(1)}, f32[256,256]{1,0:T(8,128)S(1)}, u32[]{:S(2)}, u32[]{:S(2)}) collective-permute-start(f32[256,256]{1,0:T(8,128)S(1)} %bitcast.84), channel_id=1, source_target_pairs={{0,1},{1,0},{2,3},{3,2},{4,5},{5,4},{6,7},{7,6},{8,9},{9,8},{10,11... | collective-permute-start | bytes 786440 | tf_op jit(solution)/shard_map/ppermute | solution.py:23
  87.5 7.4 %collective-permute-done.6 = f32[256,256]{1,0:T(8,128)S(1)} collective-permute-done((f32[256,256]{1,0:T(8,128)S(1)}, f32[256,256]{1,0:T(8,128)S(1)}, u32[]{:S(2)}, u32[]{:S(2)}) %collective-permute-start.6) | collective-permute-done | bytes 262176 | tf_op jit(solution)/shard_map/ppermute | solution.py:23
  95.0 1.2 fusion.1
  96.1 3.0 %collective-permute-start.9 = (f32[512,1024]{1,0:T(8,128)S(1)}, f32[512,1024]{1,0:T(8,128)S(1)}, u32[]{:S(2)}, u32[]{:S(2)}) collective-permute-start(f32[512,1024]{1,0:T(8,128)S(1)} %fusion.1), channel_id=1, source_target_pairs={{0,64},{64,0},{1,65},{65,1},{2,66},{66,2},{3,67},{67,3},{4,68},{68... | collective-permute-start | bytes 6291464 | tf_op jit(solution)/shard_map/ppermute | solution.py:23
  99.1 2.0 %collective-permute-start.8 = (f32[256,256]{1,0:T(8,128)S(1)}, f32[256,256]{1,0:T(8,128)S(1)}, u32[]{:S(2)}, u32[]{:S(2)}) collective-permute-start(f32[256,256]{1,0:T(8,128)S(1)} %bitcast.82), channel_id=1, source_target_pairs={{0,1},{1,0},{2,3},{3,2},{4,5},{5,4},{6,7},{7,6},{8,9},{9,8},{10,11... | collective-permute-start | bytes 786440 | tf_op jit(solution)/shard_map/ppermute | solution.py:23
  101.2 3.6 %fusion.17 = f32[256,1024]{1,0:T(8,128)} fusion(f32[512,256]{1,0:T(8,128)S(1)} %bitcast.81, f32[512,1024]{1,0:T(8,128)} %bitcast.2.words_ref), kind=kOutput, calls=%fused_computation.51 | convolution fusion | flops 805306368 | bytes 3670016 | tf_op jit(solution)/shard_map/dot_general | solution.py:41
  104.8 4.1 %collective-permute-done.8 = f32[256,256]{1,0:T(8,128)S(1)} collective-permute-done((f32[256,256]{1,0:T(8,128)S(1)}, f32[256,256]{1,0:T(8,128)S(1)}, u32[]{:S(2)}, u32[]{:S(2)}) %collective-permute-start.8) | collective-permute-done | bytes 262176 | tf_op jit(solution)/shard_map/ppermute | solution.py:23
  108.9 1.2 convolution_add_fusion
  110.1 30.7 %all_to_all.18 = f32[16,32,1024]{2,1,0:T(8,128)} all-to-all(f32[16,32,1024]{2,1,0:T(8,128)S(1)} %bitcast.77), channel_id=1, replica_groups=mesh['zh'=4,'core'=2,'y'=4,'x'=4,'t'=4] {'y','x'}, dimensions={0} | all-to-all | bytes 4194304 | tf_op jit(solution)/shard_map/all_to_all | solution.py:31
  140.8 1.7 reduce_sum.19
  142.5 9.1 %collective-permute-start.12 = (f32[16,1024]{1,0:T(8,128)S(1)}, f32[16,1024]{1,0:T(8,128)S(1)}, u32[]{:S(2)}, u32[]{:S(2)}) collective-permute-start(f32[16,1024]{1,0:T(8,128)S(1)} %get-tuple-element.26), channel_id=1, source_target_pairs={{0,384},{128,256},{256,128},{384,0},{1,385},{129,257},{257,129},{3... | collective-permute-start | bytes 196616 | tf_op jit(solution)/shard_map/ppermute | solution.py:23
  151.6 5.2 %collective-permute-start.10 = (f32[16,1024]{1,0:T(8,128)S(1)}, f32[16,1024]{1,0:T(8,128)S(1)}, u32[]{:S(2)}, u32[]{:S(2)}) collective-permute-start(f32[16,1024]{1,0:T(8,128)S(1)} %get-tuple-element.24), channel_id=1, source_target_pairs={{0,128},{128,0},{256,384},{384,256},{1,129},{129,1},{257,385},{385... | collective-permute-start | bytes 196616 | tf_op jit(solution)/shard_map/ppermute | solution.py:23
  156.8 3.9 %fusion = f32[256,1024]{1,0:T(8,128)} fusion(f32[256,1024]{1,0:T(8,128)} %fusion.17, f32[512,256]{1,0:T(8,128)S(1)} %bitcast.79, f32[512,1024]{1,0:T(8,128)} %collective-permute-done.1.words_ref, f32[256,1024]{1,0:T(8,128)S(1)} %copy-done.1, f32[256]{0:T(256)S(1)} %convert_divide_fusion), kind=kOutput, calls=%fused_computation.2 | convolution fusion | flops 806354944 | bytes 5768192 | tf_op jit(solution)/shard_map/dot_general | solution.py:41
  160.8 5.2 %collective-permute-start.13 = (f32[16,1024]{1,0:T(8,128)S(1)}, f32[16,1024]{1,0:T(8,128)S(1)}, u32[]{:S(2)}, u32[]{:S(2)}) collective-permute-start(f32[16,1024]{1,0:T(8,128)S(1)} %add.162), channel_id=1, source_target_pairs={{0,128},{128,0},{256,384},{384,256},{1,129},{129,1},{257,385},{385... | collective-permute-start | bytes 196616 | tf_op jit(solution)/shard_map/ppermute | solution.py:23
  165.9 4.2 %collective-permute-start.11 = (f32[16,1024]{1,0:T(8,128)S(1)}, f32[16,1024]{1,0:T(8,128)S(1)}, u32[]{:S(2)}, u32[]{:S(2)}) collective-permute-start(f32[16,1024]{1,0:T(8,128)S(1)} %add.160), channel_id=1, source_target_pairs={{0,384},{128,256},{256,128},{384,0},{1,385},{129,257},{257,129},{3... | collective-permute-start | bytes 196616 | tf_op jit(solution)/shard_map/ppermute | solution.py:23
  170.2 5.5 %collective-permute-done.11 = f32[16,1024]{1,0:T(8,128)S(1)} collective-permute-done((f32[16,1024]{1,0:T(8,128)S(1)}, f32[16,1024]{1,0:T(8,128)S(1)}, u32[]{:S(2)}, u32[]{:S(2)}) %collective-permute-start.11) | collective-permute-done | bytes 65568 | tf_op jit(solution)/shard_map/ppermute | solution.py:23
  175.7 6.0 %collective-permute-start.14 = (f32[32,1024]{1,0:T(8,128)S(1)}, f32[32,1024]{1,0:T(8,128)S(1)}, u32[]{:S(2)}, u32[]{:S(2)}) collective-permute-start(f32[32,1024]{1,0:T(8,128)S(1)} %get-tuple-element.30), channel_id=1, source_target_pairs={{0,64},{64,0},{1,65},{65,1},{2,66},{66,2},{3,67},{67,3},{4,68},{68... | collective-permute-start | bytes 393224 | tf_op jit(solution)/shard_map/ppermute | solution.py:23
  181.7 1.0 collective-permute-done.14
  (60 shorter events, 4.1 us)
Async XLA Ops:
  0.6 41.0 %copy-start = (s32[256,1024]{1,0:T(8,128)S(1)}, s32[256,1024]{1,0:T(8,128)}, u32[]{:S(2)}) copy-start(s32[256,1024]{1,0:T(8,128)} %param.8) | copy-start | bytes 3145732
  2.6 39.3 %copy-start.4 = (s32[1,16]{1,0:T(1,128)S(1)}, s32[1,16]{1,0:T(1,128)}, u32[]{:S(2)}) copy-start(s32[1,16]{1,0:T(1,128)} %param.9) | copy-start | bytes 196
  2.6 39.5 %copy-start.1 = (f32[256,1024]{1,0:T(8,128)S(1)}, f32[256,1024]{1,0:T(8,128)}, u32[]{:S(2)}) copy-start(f32[256,1024]{1,0:T(8,128)} %mix_ref.2) | copy-start | bytes 3145732
  36.2 12.1 %collective-permute-start.1 = (f32[512,1024]{1,0:T(8,128)}, f32[512,1024]{1,0:T(8,128)}, u32[]{:S(2)}, u32[]{:S(2)}) collective-permute-start(f32[512,1024]{1,0:T(8,128)} %bitcast.2.words_ref), channel_id=1, source_target_pairs={{0,64},{64,0},{1,65},{65,1},{2,66},{66,2},{3,67},{67,3},{4,68},{68... | collective-permute-start | bytes 6291464 | tf_op jit(solution)/shard_map/ppermute | solution.py:23
  44.9 10.1 %collective-permute-start = (f32[2,136,256]{2,1,0:T(8,128)S(1)}, f32[2,136,256]{2,1,0:T(8,128)S(1)}, u32[]{:S(2)}, u32[]{:S(2)}) collective-permute-start(f32[2,136,256]{2,1,0:T(8,128)S(1)} %dynamic-slice_bitcast_fusion.1), channel_id=1, source_target_pairs={{0,1},{1,0},{2,3},{3,2},{4,5},{5,4},{6,7},{7,6},{8,9},{9,8},{10,11... | collective-permute-start | bytes 835592 | tf_op jit(solution)/shard_map/ppermute | solution.py:23
  50.9 16.9 %copy-start.3 = (s32[256]{0:T(256)S(1)}, s32[256]{0:T(256)}, u32[]{:S(2)}) copy-start(s32[256]{0:T(256)} %param.7) | copy-start | bytes 3076
  51.0 9.8 %collective-permute-start.3 = (f32[2,136,256]{2,1,0:T(8,128)S(1)}, f32[2,136,256]{2,1,0:T(8,128)S(1)}, u32[]{:S(2)}, u32[]{:S(2)}) collective-permute-start(f32[2,136,256]{2,1,0:T(8,128)S(1)} %dynamic-slice_bitcast_fusion), channel_id=1, source_target_pairs={{0,1},{1,0},{2,3},{3,2},{4,5},{5,4},{6,7},{7,6},{8,9},{9,8},{10,11... | collective-permute-start | bytes 835592 | tf_op jit(solution)/shard_map/ppermute | solution.py:23
  55.1 8.6 %collective-permute-start.2 = (f32[136,256]{1,0:T(8,128)S(1)}, f32[136,256]{1,0:T(8,128)S(1)}, u32[]{:S(2)}, u32[]{:S(2)}) collective-permute-start(f32[136,256]{1,0:T(8,128)S(1)} %dynamic-slice_bitcast_fusion.3), channel_id=1, source_target_pairs={{0,2},{1,3},{2,0},{3,1},{4,6},{5,7},{6,4},{7,5},{8,10},{9,11},{10,... | collective-permute-start | bytes 417800 | tf_op jit(solution)/shard_map/ppermute | solution.py:23
  63.7 6.7 %collective-permute-start.5 = (f32[136,256]{1,0:T(8,128)S(1)}, f32[136,256]{1,0:T(8,128)S(1)}, u32[]{:S(2)}, u32[]{:S(2)}) collective-permute-start(f32[136,256]{1,0:T(8,128)S(1)} %dynamic-slice_bitcast_fusion.2), channel_id=1, source_target_pairs={{0,2},{1,3},{2,0},{3,1},{4,6},{5,7},{6,4},{7,5},{8,10},{9,11},{10,... | collective-permute-start | bytes 417800 | tf_op jit(solution)/shard_map/ppermute | solution.py:23
  67.9 13.7 %collective-permute-start.4 = (f32[128,256]{1,0:T(8,128)S(1)}, f32[128,256]{1,0:T(8,128)S(1)}, u32[]{:S(2)}, u32[]{:S(2)}) collective-permute-start(f32[128,256]{1,0:T(8,128)S(1)} %get-tuple-element.35), channel_id=1, source_target_pairs={{0,2},{1,3},{2,0},{3,1},{4,6},{5,7},{6,4},{7,5},{8,10},{9,11},{10,... | collective-permute-start | bytes 393224 | tf_op jit(solution)/shard_map/ppermute | solution.py:23
  70.6 16.9 %collective-permute-start.7 = (f32[128,256]{1,0:T(8,128)S(1)}, f32[128,256]{1,0:T(8,128)S(1)}, u32[]{:S(2)}, u32[]{:S(2)}) collective-permute-start(f32[128,256]{1,0:T(8,128)S(1)} %get-tuple-element.37), channel_id=1, source_target_pairs={{0,2},{1,3},{2,0},{3,1},{4,6},{5,7},{6,4},{7,5},{8,10},{9,11},{10,... | collective-permute-start | bytes 393224 | tf_op jit(solution)/shard_map/ppermute | solution.py:23
  81.7 13.3 %collective-permute-start.6 = (f32[256,256]{1,0:T(8,128)S(1)}, f32[256,256]{1,0:T(8,128)S(1)}, u32[]{:S(2)}, u32[]{:S(2)}) collective-permute-start(f32[256,256]{1,0:T(8,128)S(1)} %bitcast.84), channel_id=1, source_target_pairs={{0,1},{1,0},{2,3},{3,2},{4,5},{5,4},{6,7},{7,6},{8,9},{9,8},{10,11... | collective-permute-start | bytes 786440 | tf_op jit(solution)/shard_map/ppermute | solution.py:23
  96.1 12.8 %collective-permute-start.9 = (f32[512,1024]{1,0:T(8,128)S(1)}, f32[512,1024]{1,0:T(8,128)S(1)}, u32[]{:S(2)}, u32[]{:S(2)}) collective-permute-start(f32[512,1024]{1,0:T(8,128)S(1)} %fusion.1), channel_id=1, source_target_pairs={{0,64},{64,0},{1,65},{65,1},{2,66},{66,2},{3,67},{67,3},{4,68},{68... | collective-permute-start | bytes 6291464 | tf_op jit(solution)/shard_map/ppermute | solution.py:23
  99.1 9.7 %collective-permute-start.8 = (f32[256,256]{1,0:T(8,128)S(1)}, f32[256,256]{1,0:T(8,128)S(1)}, u32[]{:S(2)}, u32[]{:S(2)}) collective-permute-start(f32[256,256]{1,0:T(8,128)S(1)} %bitcast.82), channel_id=1, source_target_pairs={{0,1},{1,0},{2,3},{3,2},{4,5},{5,4},{6,7},{7,6},{8,9},{9,8},{10,11... | collective-permute-start | bytes 786440 | tf_op jit(solution)/shard_map/ppermute | solution.py:23
  142.5 40.2 %copy-start.2 = (f32[64,1024]{1,0:T(8,128)S(1)}, f32[64,1024]{1,0:T(8,128)}, u32[]{:S(2)}) copy-start(f32[64,1024]{1,0:T(8,128)} %param.10) | copy-start | bytes 786436
  142.5 18.2 %collective-permute-start.12 = (f32[16,1024]{1,0:T(8,128)S(1)}, f32[16,1024]{1,0:T(8,128)S(1)}, u32[]{:S(2)}, u32[]{:S(2)}) collective-permute-start(f32[16,1024]{1,0:T(8,128)S(1)} %get-tuple-element.26), channel_id=1, source_target_pairs={{0,384},{128,256},{256,128},{384,0},{1,385},{129,257},{257,129},{3... | collective-permute-start | bytes 196616 | tf_op jit(solution)/shard_map/ppermute | solution.py:23
  151.6 9.1 %collective-permute-start.10 = (f32[16,1024]{1,0:T(8,128)S(1)}, f32[16,1024]{1,0:T(8,128)S(1)}, u32[]{:S(2)}, u32[]{:S(2)}) collective-permute-start(f32[16,1024]{1,0:T(8,128)S(1)} %get-tuple-element.24), channel_id=1, source_target_pairs={{0,128},{128,0},{256,384},{384,256},{1,129},{129,1},{257,385},{385... | collective-permute-start | bytes 196616 | tf_op jit(solution)/shard_map/ppermute | solution.py:23
  160.8 9.4 %collective-permute-start.13 = (f32[16,1024]{1,0:T(8,128)S(1)}, f32[16,1024]{1,0:T(8,128)S(1)}, u32[]{:S(2)}, u32[]{:S(2)}) collective-permute-start(f32[16,1024]{1,0:T(8,128)S(1)} %add.162), channel_id=1, source_target_pairs={{0,128},{128,0},{256,384},{384,256},{1,129},{129,1},{257,385},{385... | collective-permute-start | bytes 196616 | tf_op jit(solution)/shard_map/ppermute | solution.py:23
  165.9 9.7 %collective-permute-start.11 = (f32[16,1024]{1,0:T(8,128)S(1)}, f32[16,1024]{1,0:T(8,128)S(1)}, u32[]{:S(2)}, u32[]{:S(2)}) collective-permute-start(f32[16,1024]{1,0:T(8,128)S(1)} %add.160), channel_id=1, source_target_pairs={{0,384},{128,256},{256,128},{384,0},{1,385},{129,257},{257,129},{3... | collective-permute-start | bytes 196616 | tf_op jit(solution)/shard_map/ppermute | solution.py:23
  175.7 7.0 %collective-permute-start.14 = (f32[32,1024]{1,0:T(8,128)S(1)}, f32[32,1024]{1,0:T(8,128)S(1)}, u32[]{:S(2)}, u32[]{:S(2)}) collective-permute-start(f32[32,1024]{1,0:T(8,128)S(1)} %get-tuple-element.30), channel_id=1, source_target_pairs={{0,64},{64,0},{1,65},{65,1},{2,66},{66,2},{3,67},{67,3},{4,68},{68... | collective-permute-start | bytes 393224 | tf_op jit(solution)/shard_map/ppermute | solution.py:23

commit v5 on v4

--- a/solution.py
+++ b/solution.py
@@ -178,14 +178,13 @@
     sums_0 = matmul(ratio_0, doc_weight, by_doc)
     sums_given = moved(sums_0, "core", first_partner)
     by_word = ((0,), (0,))
-    doc_sums = matmul(ratio_0, words[0], by_word)
-    ratio_1 = joined(half_1, after(arrived_1, doc_sums), low)
+    ratio_1 = joined(half_1, after(arrived_1, sums_0), low)
 
     sums = scattered(matmul(ratio_1, doc_weight, by_doc) + sums_given, cut)
     own_a, own_b = lax.optimization_barrier((sums[: half // 2], sums[half // 2 :]))
     arrived_a = moved(own_a, "zh", first_partner)
     arrived_b = moved(own_b, "zh", across)
-    doc_topic = doc_weight * (doc_sums + matmul(ratio_1, words[1], by_word))
+    doc_topic = doc_weight * (matmul(ratio_0, words[0], by_word) + matmul(ratio_1, words[1], by_word))
     own_a = own_a + after(arrived_a, doc_topic)
     arrived_a = moved(own_a, "zh", across)
     own_b = own_b + after(arrived_b, own_a)

time: 184 us -> 190 us (1.033)
  waiting for transfers between devices: 30.9 us -> 62.2 us
  blocking collectives: 64.3 us -> 33.6 us
  starting transfers between devices: 66.3 us -> 70.3 us
    all_to_all x2 -> x1, blocking collectives: 64.3 us -> 33.6 us  [exchanged(): return lax.all_to_all(blocks, axes, 0, 0, tiled=True)]
    all_to_all x0 -> x1, waiting for transfers between devices: none -> 27.6 us  [exchanged(): return lax.all_to_all(blocks, axes, 0, 0, tiled=True)]
    all_to_all x0 -> x1, starting transfers between devices: none -> 4.44 us  [exchanged(): return lax.all_to_all(blocks, axes, 0, 0, tiled=True)]
    ppermute x15, waiting for transfers between devices: 30.9 us -> 34.6 us  [moved(): lax.ppermute(block, axis, [(i, partner(i)) for i in range(lax.axis_size(a...]
  transfers between devices with their start and end apart: 15 -> 16, of which waited for: 9 -> 10; matrix products, arithmetic and copies ran while one was open for 5% -> 5% of each run, Pallas kernels for 3% -> 3%
where the time goes in v5:
time: 190 us
  starting transfers between devices  70.3 us (37%)
  waiting for transfers between devices  62.2 us (33%)
  blocking collectives  33.6 us (18%)
  matrix products  11.3 us (6%)
  Pallas kernels  5.1 us (3%)
  other arithmetic  4.78 us (3%)
    ppermute x15, starting transfers between devices, moved(): lax.ppermute(block, axis, [(i, partner(i)) for i in range(lax.axis_size(a...  65.9 us
    ppermute x15, waiting for transfers between devices, moved(): lax.ppermute(block, axis, [(i, partner(i)) for i in range(lax.axis_size(a...  34.6 us
    all_to_all x1, blocking collectives, exchanged(): return lax.all_to_all(blocks, axes, 0, 0, tiled=True)  33.6 us
    all_to_all x1, waiting for transfers between devices, exchanged(): return lax.all_to_all(blocks, axes, 0, 0, tiled=True)  27.6 us
    dot_general x4, matrix products, matmul(): lax.dot_general(left, right, (contract, ((), ())), precision=lax.Precisio...  11.3 us
    pallas_call x2, Pallas kernels, parts_of_words(): pl.pallas_call(parts_kernel, out_shape=jax.ShapeDtypeStruct((chunks, chun...  5.1 us
    all_to_all x1, starting transfers between devices, exchanged(): return lax.all_to_all(blocks, axes, 0, 0, tiled=True)  4.44 us
  transfers between devices with their start and end apart: 16, of which 10 were waited for; matrix products, arithmetic and copies ran while one was open for 5% of the time, Pallas kernels for 3%

profile of v5, /device:TPU:1, one launch (start us, length us, event | category | flops | bytes accessed | tf_op | source)
XLA Modules:
  0.0 189.6 jit_solution(17897600742978153451)
XLA Ops:
  2.6 33.6 %all_to_all.17 = f32[16,32,1024]{2,1,0:T(8,128)} all-to-all(f32[16,32,1024]{2,1,0:T(8,128)S(1)} %broadcast_in_dim.42), channel_id=1, replica_groups=mesh['zh'=4,'core'=2,'y'=4,'x'=4,'t'=4] {'y','x'}, dimensions={0} | all-to-all | bytes 4194304 | tf_op jit(solution)/shard_map/all_to_all | solution.py:31
  36.2 5.4 %collective-permute-start.1 = (f32[512,1024]{1,0:T(8,128)}, f32[512,1024]{1,0:T(8,128)}, u32[]{:S(2)}, u32[]{:S(2)}) collective-permute-start(f32[512,1024]{1,0:T(8,128)} %bitcast.2.words_ref), channel_id=1, source_target_pairs={{0,64},{64,0},{1,65},{65,1},{2,66},{66,2},{3,67},{67,3},{4,68},{68... | collective-permute-start | bytes 6291464 | tf_op jit(solution)/shard_map/ppermute | solution.py:23
  42.3 2.6 %shard_map.77 = f32[4,136,256]{2,1,0:T(8,128)S(1)} custom-call(f32[512,1024]{1,0:T(8,128)} %bitcast.2.words_ref, f32[256,1024]{1,0:T(8,128)S(1)} %copy-done.1, f32[1,256]{1,0:T(1,128)S(1)} %bitcast.75), custom_call_target="tpu_custom_call" | custom-call | flops 805306368 | bytes 3145728 | tf_op jit(solution)/shard_map/pallas_call | solution.py:79
  44.9 3.4 %collective-permute-start = (f32[2,136,256]{2,1,0:T(8,128)S(1)}, f32[2,136,256]{2,1,0:T(8,128)S(1)}, u32[]{:S(2)}, u32[]{:S(2)}) collective-permute-start(f32[2,136,256]{2,1,0:T(8,128)S(1)} %dynamic-slice_bitcast_fusion.1), channel_id=1, source_target_pairs={{0,1},{1,0},{2,3},{3,2},{4,5},{5,4},{6,7},{7,6},{8,9},{9,8},{10,11... | collective-permute-start | bytes 835592 | tf_op jit(solution)/shard_map/ppermute | solution.py:23
  48.4 2.6 %shard_map.78 = f32[4,136,256]{2,1,0:T(8,128)S(1)} custom-call(f32[512,1024]{1,0:T(8,128)} %collective-permute-done.1.words_ref, f32[256,1024]{1,0:T(8,128)S(1)} %copy-done.1, f32[1,256]{1,0:T(1,128)S(1)} %bitcast.76), custom_call_target="tpu_custom_call" | custom-call | flops 805306368 | bytes 3145728 | tf_op jit(solution)/shard_map/pallas_call | solution.py:79
  51.0 1.9 %collective-permute-start.3 = (f32[2,136,256]{2,1,0:T(8,128)S(1)}, f32[2,136,256]{2,1,0:T(8,128)S(1)}, u32[]{:S(2)}, u32[]{:S(2)}) collective-permute-start(f32[2,136,256]{2,1,0:T(8,128)S(1)} %dynamic-slice_bitcast_fusion), channel_id=1, source_target_pairs={{0,1},{1,0},{2,3},{3,2},{4,5},{5,4},{6,7},{7,6},{8,9},{9,8},{10,11... | collective-permute-start | bytes 835592 | tf_op jit(solution)/shard_map/ppermute | solution.py:23
  52.9 2.2 %collective-permute-done = f32[2,136,256]{2,1,0:T(8,128)S(1)} collective-permute-done((f32[2,136,256]{2,1,0:T(8,128)S(1)}, f32[2,136,256]{2,1,0:T(8,128)S(1)}, u32[]{:S(2)}, u32[]{:S(2)}) %collective-permute-start) | collective-permute-done | bytes 278560 | tf_op jit(solution)/shard_map/ppermute | solution.py:23
  55.1 5.1 %collective-permute-start.2 = (f32[136,256]{1,0:T(8,128)S(1)}, f32[136,256]{1,0:T(8,128)S(1)}, u32[]{:S(2)}, u32[]{:S(2)}) collective-permute-start(f32[136,256]{1,0:T(8,128)S(1)} %dynamic-slice_bitcast_fusion.3), channel_id=1, source_target_pairs={{0,2},{1,3},{2,0},{3,1},{4,6},{5,7},{6,4},{7,5},{8,10},{9,11},{10,... | collective-permute-start | bytes 417800 | tf_op jit(solution)/shard_map/ppermute | solution.py:23
  60.8 2.9 %collective-permute-done.2 = f32[136,256]{1,0:T(8,128)S(1)} collective-permute-done((f32[136,256]{1,0:T(8,128)S(1)}, f32[136,256]{1,0:T(8,128)S(1)}, u32[]{:S(2)}, u32[]{:S(2)}) %collective-permute-start.2) | collective-permute-done | bytes 139296 | tf_op jit(solution)/shard_map/ppermute | solution.py:23
  63.7 4.0 %collective-permute-start.5 = (f32[136,256]{1,0:T(8,128)S(1)}, f32[136,256]{1,0:T(8,128)S(1)}, u32[]{:S(2)}, u32[]{:S(2)}) collective-permute-start(f32[136,256]{1,0:T(8,128)S(1)} %dynamic-slice_bitcast_fusion.2), channel_id=1, source_target_pairs={{0,2},{1,3},{2,0},{3,1},{4,6},{5,7},{6,4},{7,5},{8,10},{9,11},{10,... | collective-permute-start | bytes 417800 | tf_op jit(solution)/shard_map/ppermute | solution.py:23
  67.9 2.1 %collective-permute-start.4 = (f32[128,256]{1,0:T(8,128)S(1)}, f32[128,256]{1,0:T(8,128)S(1)}, u32[]{:S(2)}, u32[]{:S(2)}) collective-permute-start(f32[128,256]{1,0:T(8,128)S(1)} %get-tuple-element.35), channel_id=1, source_target_pairs={{0,2},{1,3},{2,0},{3,1},{4,6},{5,7},{6,4},{7,5},{8,10},{9,11},{10,... | collective-permute-start | bytes 393224 | tf_op jit(solution)/shard_map/ppermute | solution.py:23
  70.6 4.0 %collective-permute-start.7 = (f32[128,256]{1,0:T(8,128)S(1)}, f32[128,256]{1,0:T(8,128)S(1)}, u32[]{:S(2)}, u32[]{:S(2)}) collective-permute-start(f32[128,256]{1,0:T(8,128)S(1)} %get-tuple-element.37), channel_id=1, source_target_pairs={{0,2},{1,3},{2,0},{3,1},{4,6},{5,7},{6,4},{7,5},{8,10},{9,11},{10,... | collective-permute-start | bytes 393224 | tf_op jit(solution)/shard_map/ppermute | solution.py:23
  74.6 7.0 %collective-permute-done.4 = f32[128,256]{1,0:T(8,128)S(1)} collective-permute-done((f32[128,256]{1,0:T(8,128)S(1)}, f32[128,256]{1,0:T(8,128)S(1)}, u32[]{:S(2)}, u32[]{:S(2)}) %collective-permute-start.4) | collective-permute-done | bytes 131104 | tf_op jit(solution)/shard_map/ppermute | solution.py:23
  81.7 5.7 %collective-permute-start.6 = (f32[256,256]{1,0:T(8,128)S(1)}, f32[256,256]{1,0:T(8,128)S(1)}, u32[]{:S(2)}, u32[]{:S(2)}) collective-permute-start(f32[256,256]{1,0:T(8,128)S(1)} %bitcast.84), channel_id=1, source_target_pairs={{0,1},{1,0},{2,3},{3,2},{4,5},{5,4},{6,7},{7,6},{8,9},{9,8},{10,11... | collective-permute-start | bytes 786440 | tf_op jit(solution)/shard_map/ppermute | solution.py:23
  87.5 7.4 %collective-permute-done.6 = f32[256,256]{1,0:T(8,128)S(1)} collective-permute-done((f32[256,256]{1,0:T(8,128)S(1)}, f32[256,256]{1,0:T(8,128)S(1)}, u32[]{:S(2)}, u32[]{:S(2)}) %collective-permute-start.6) | collective-permute-done | bytes 262176 | tf_op jit(solution)/shard_map/ppermute | solution.py:23
  95.0 1.2 fusion.1
  96.1 3.0 %collective-permute-start.9 = (f32[512,1024]{1,0:T(8,128)S(1)}, f32[512,1024]{1,0:T(8,128)S(1)}, u32[]{:S(2)}, u32[]{:S(2)}) collective-permute-start(f32[512,1024]{1,0:T(8,128)S(1)} %fusion.1), channel_id=1, source_target_pairs={{0,64},{64,0},{1,65},{65,1},{2,66},{66,2},{3,67},{67,3},{4,68},{68... | collective-permute-start | bytes 6291464 | tf_op jit(solution)/shard_map/ppermute | solution.py:23
  99.1 2.0 %collective-permute-start.8 = (f32[256,256]{1,0:T(8,128)S(1)}, f32[256,256]{1,0:T(8,128)S(1)}, u32[]{:S(2)}, u32[]{:S(2)}) collective-permute-start(f32[256,256]{1,0:T(8,128)S(1)} %bitcast.82), channel_id=1, source_target_pairs={{0,1},{1,0},{2,3},{3,2},{4,5},{5,4},{6,7},{7,6},{8,9},{9,8},{10,11... | collective-permute-start | bytes 786440 | tf_op jit(solution)/shard_map/ppermute | solution.py:23
  101.2 7.7 %collective-permute-done.8 = f32[256,256]{1,0:T(8,128)S(1)} collective-permute-done((f32[256,256]{1,0:T(8,128)S(1)}, f32[256,256]{1,0:T(8,128)S(1)}, u32[]{:S(2)}, u32[]{:S(2)}) %collective-permute-start.8) | collective-permute-done | bytes 262176 | tf_op jit(solution)/shard_map/ppermute | solution.py:23
  108.9 2.6 %convolution_add_fusion = f32[512,1024]{1,0:T(8,128)} fusion(f32[512,1024]{1,0:T(8,128)S(1)} %collective-permute-done.9, f32[512,256]{1,0:T(8,128)S(1)} %bitcast.78, f32[256,1024]{1,0:T(8,128)S(1)} %copy-done.1, f32[256]{0:T(256)S(1)} %convert_divide_fusion), kind=kOutput, calls=%fused_computation | convolution fusion | flops 806354944 | bytes 5768192 | tf_op jit(solution)/shard_map/dot_general | solution.py:41
  111.5 4.4 %all-to-all-start.1 = ((f32[16,32,1024]{2,1,0:T(8,128)}), f32[16,32,1024]{2,1,0:T(8,128)}, u32[]{:S(2)}, u32[]{:S(2)}) async-start(f32[16,32,1024]{2,1,0:T(8,128)} %bitcast.77), calls=%async_computation.1 | async-start | bytes 4194304 | tf_op jit(solution)/shard_map/all_to_all | solution.py:31
  116.0 3.6 %fusion.17 = f32[256,1024]{1,0:T(8,128)} fusion(f32[512,256]{1,0:T(8,128)S(1)} %bitcast.81, f32[512,1024]{1,0:T(8,128)} %bitcast.2.words_ref), kind=kOutput, calls=%fused_computation.51 | convolution fusion | flops 805306368 | bytes 3670016 | tf_op jit(solution)/shard_map/dot_general | solution.py:41
  119.6 27.6 %all-to-all-done.1 = f32[16,32,1024]{2,1,0:T(8,128)} async-done(((f32[16,32,1024]{2,1,0:T(8,128)}), f32[16,32,1024]{2,1,0:T(8,128)}, u32[]{:S(2)}, u32[]{:S(2)}) %all-to-all-start.1) | async-done | bytes 2097184 | tf_op jit(solution)/shard_map/all_to_all | solution.py:31
  147.2 1.7 reduce_sum.19
  148.9 9.1 %collective-permute-start.12 = (f32[16,1024]{1,0:T(8,128)S(1)}, f32[16,1024]{1,0:T(8,128)S(1)}, u32[]{:S(2)}, u32[]{:S(2)}) collective-permute-start(f32[16,1024]{1,0:T(8,128)S(1)} %get-tuple-element.26), channel_id=1, source_target_pairs={{0,384},{128,256},{256,128},{384,0},{1,385},{129,257},{257,129},{3... | collective-permute-start | bytes 196616 | tf_op jit(solution)/shard_map/ppermute | solution.py:23
  158.0 5.2 %collective-permute-start.10 = (f32[16,1024]{1,0:T(8,128)S(1)}, f32[16,1024]{1,0:T(8,128)S(1)}, u32[]{:S(2)}, u32[]{:S(2)}) collective-permute-start(f32[16,1024]{1,0:T(8,128)S(1)} %get-tuple-element.24), channel_id=1, source_target_pairs={{0,128},{128,0},{256,384},{384,256},{1,129},{129,1},{257,385},{385... | collective-permute-start | bytes 196616 | tf_op jit(solution)/shard_map/ppermute | solution.py:23
  163.2 3.9 %fusion = f32[256,1024]{1,0:T(8,128)} fusion(f32[256,1024]{1,0:T(8,128)} %fusion.17, f32[512,256]{1,0:T(8,128)S(1)} %bitcast.79, f32[512,1024]{1,0:T(8,128)} %collective-permute-done.1.words_ref, f32[256,1024]{1,0:T(8,128)S(1)} %copy-done.1, f32[256]{0:T(256)S(1)} %convert_divide_fusion), kind=kOutput, calls=%fused_computation.2 | convolution fusion | flops 806354944 | bytes 5768192 | tf_op jit(solution)/shard_map/dot_general | solution.py:41
  167.2 5.3 %collective-permute-start.13 = (f32[16,1024]{1,0:T(8,128)S(1)}, f32[16,1024]{1,0:T(8,128)S(1)}, u32[]{:S(2)}, u32[]{:S(2)}) collective-permute-start(f32[16,1024]{1,0:T(8,128)S(1)} %add.162), channel_id=1, source_target_pairs={{0,128},{128,0},{256,384},{384,256},{1,129},{129,1},{257,385},{385... | collective-permute-start | bytes 196616 | tf_op jit(solution)/shard_map/ppermute | solution.py:23
  172.4 4.1 %collective-permute-start.11 = (f32[16,1024]{1,0:T(8,128)S(1)}, f32[16,1024]{1,0:T(8,128)S(1)}, u32[]{:S(2)}, u32[]{:S(2)}) collective-permute-start(f32[16,1024]{1,0:T(8,128)S(1)} %add.160), channel_id=1, source_target_pairs={{0,384},{128,256},{256,128},{384,0},{1,385},{129,257},{257,129},{3... | collective-permute-start | bytes 196616 | tf_op jit(solution)/shard_map/ppermute | solution.py:23
  176.6 5.6 %collective-permute-done.11 = f32[16,1024]{1,0:T(8,128)S(1)} collective-permute-done((f32[16,1024]{1,0:T(8,128)S(1)}, f32[16,1024]{1,0:T(8,128)S(1)}, u32[]{:S(2)}, u32[]{:S(2)}) %collective-permute-start.11) | collective-permute-done | bytes 65568 | tf_op jit(solution)/shard_map/ppermute | solution.py:23
  182.2 5.6 %collective-permute-start.14 = (f32[32,1024]{1,0:T(8,128)S(1)}, f32[32,1024]{1,0:T(8,128)S(1)}, u32[]{:S(2)}, u32[]{:S(2)}) collective-permute-start(f32[32,1024]{1,0:T(8,128)S(1)} %get-tuple-element.30), channel_id=1, source_target_pairs={{0,64},{64,0},{1,65},{65,1},{2,66},{66,2},{3,67},{67,3},{4,68},{68... | collective-permute-start | bytes 393224 | tf_op jit(solution)/shard_map/ppermute | solution.py:23
  187.8 1.0 collective-permute-done.14
  (61 shorter events, 5.0 us)
Async XLA Ops:
  0.6 41.0 %copy-start = (s32[256,1024]{1,0:T(8,128)S(1)}, s32[256,1024]{1,0:T(8,128)}, u32[]{:S(2)}) copy-start(s32[256,1024]{1,0:T(8,128)} %param.8) | copy-start | bytes 3145732
  2.6 39.3 %copy-start.4 = (s32[1,16]{1,0:T(1,128)S(1)}, s32[1,16]{1,0:T(1,128)}, u32[]{:S(2)}) copy-start(s32[1,16]{1,0:T(1,128)} %param.9) | copy-start | bytes 196
  2.6 39.5 %copy-start.1 = (f32[256,1024]{1,0:T(8,128)S(1)}, f32[256,1024]{1,0:T(8,128)}, u32[]{:S(2)}) copy-start(f32[256,1024]{1,0:T(8,128)} %mix_ref.2) | copy-start | bytes 3145732
  36.2 12.1 %collective-permute-start.1 = (f32[512,1024]{1,0:T(8,128)}, f32[512,1024]{1,0:T(8,128)}, u32[]{:S(2)}, u32[]{:S(2)}) collective-permute-start(f32[512,1024]{1,0:T(8,128)} %bitcast.2.words_ref), channel_id=1, source_target_pairs={{0,64},{64,0},{1,65},{65,1},{2,66},{66,2},{3,67},{67,3},{4,68},{68... | collective-permute-start | bytes 6291464 | tf_op jit(solution)/shard_map/ppermute | solution.py:23
  44.9 10.1 %collective-permute-start = (f32[2,136,256]{2,1,0:T(8,128)S(1)}, f32[2,136,256]{2,1,0:T(8,128)S(1)}, u32[]{:S(2)}, u32[]{:S(2)}) collective-permute-start(f32[2,136,256]{2,1,0:T(8,128)S(1)} %dynamic-slice_bitcast_fusion.1), channel_id=1, source_target_pairs={{0,1},{1,0},{2,3},{3,2},{4,5},{5,4},{6,7},{7,6},{8,9},{9,8},{10,11... | collective-permute-start | bytes 835592 | tf_op jit(solution)/shard_map/ppermute | solution.py:23
  50.9 16.9 %copy-start.3 = (s32[256]{0:T(256)S(1)}, s32[256]{0:T(256)}, u32[]{:S(2)}) copy-start(s32[256]{0:T(256)} %param.7) | copy-start | bytes 3076
  51.0 9.8 %collective-permute-start.3 = (f32[2,136,256]{2,1,0:T(8,128)S(1)}, f32[2,136,256]{2,1,0:T(8,128)S(1)}, u32[]{:S(2)}, u32[]{:S(2)}) collective-permute-start(f32[2,136,256]{2,1,0:T(8,128)S(1)} %dynamic-slice_bitcast_fusion), channel_id=1, source_target_pairs={{0,1},{1,0},{2,3},{3,2},{4,5},{5,4},{6,7},{7,6},{8,9},{9,8},{10,11... | collective-permute-start | bytes 835592 | tf_op jit(solution)/shard_map/ppermute | solution.py:23
  55.1 8.6 %collective-permute-start.2 = (f32[136,256]{1,0:T(8,128)S(1)}, f32[136,256]{1,0:T(8,128)S(1)}, u32[]{:S(2)}, u32[]{:S(2)}) collective-permute-start(f32[136,256]{1,0:T(8,128)S(1)} %dynamic-slice_bitcast_fusion.3), channel_id=1, source_target_pairs={{0,2},{1,3},{2,0},{3,1},{4,6},{5,7},{6,4},{7,5},{8,10},{9,11},{10,... | collective-permute-start | bytes 417800 | tf_op jit(solution)/shard_map/ppermute | solution.py:23
  63.7 6.7 %collective-permute-start.5 = (f32[136,256]{1,0:T(8,128)S(1)}, f32[136,256]{1,0:T(8,128)S(1)}, u32[]{:S(2)}, u32[]{:S(2)}) collective-permute-start(f32[136,256]{1,0:T(8,128)S(1)} %dynamic-slice_bitcast_fusion.2), channel_id=1, source_target_pairs={{0,2},{1,3},{2,0},{3,1},{4,6},{5,7},{6,4},{7,5},{8,10},{9,11},{10,... | collective-permute-start | bytes 417800 | tf_op jit(solution)/shard_map/ppermute | solution.py:23
  67.9 13.7 %collective-permute-start.4 = (f32[128,256]{1,0:T(8,128)S(1)}, f32[128,256]{1,0:T(8,128)S(1)}, u32[]{:S(2)}, u32[]{:S(2)}) collective-permute-start(f32[128,256]{1,0:T(8,128)S(1)} %get-tuple-element.35), channel_id=1, source_target_pairs={{0,2},{1,3},{2,0},{3,1},{4,6},{5,7},{6,4},{7,5},{8,10},{9,11},{10,... | collective-permute-start | bytes 393224 | tf_op jit(solution)/shard_map/ppermute | solution.py:23
  70.6 16.9 %collective-permute-start.7 = (f32[128,256]{1,0:T(8,128)S(1)}, f32[128,256]{1,0:T(8,128)S(1)}, u32[]{:S(2)}, u32[]{:S(2)}) collective-permute-start(f32[128,256]{1,0:T(8,128)S(1)} %get-tuple-element.37), channel_id=1, source_target_pairs={{0,2},{1,3},{2,0},{3,1},{4,6},{5,7},{6,4},{7,5},{8,10},{9,11},{10,... | collective-permute-start | bytes 393224 | tf_op jit(solution)/shard_map/ppermute | solution.py:23
  81.7 13.3 %collective-permute-start.6 = (f32[256,256]{1,0:T(8,128)S(1)}, f32[256,256]{1,0:T(8,128)S(1)}, u32[]{:S(2)}, u32[]{:S(2)}) collective-permute-start(f32[256,256]{1,0:T(8,128)S(1)} %bitcast.84), channel_id=1, source_target_pairs={{0,1},{1,0},{2,3},{3,2},{4,5},{5,4},{6,7},{7,6},{8,9},{9,8},{10,11... | collective-permute-start | bytes 786440 | tf_op jit(solution)/shard_map/ppermute | solution.py:23
  96.1 12.8 %collective-permute-start.9 = (f32[512,1024]{1,0:T(8,128)S(1)}, f32[512,1024]{1,0:T(8,128)S(1)}, u32[]{:S(2)}, u32[]{:S(2)}) collective-permute-start(f32[512,1024]{1,0:T(8,128)S(1)} %fusion.1), channel_id=1, source_target_pairs={{0,64},{64,0},{1,65},{65,1},{2,66},{66,2},{3,67},{67,3},{4,68},{68... | collective-permute-start | bytes 6291464 | tf_op jit(solution)/shard_map/ppermute | solution.py:23
  99.1 9.7 %collective-permute-start.8 = (f32[256,256]{1,0:T(8,128)S(1)}, f32[256,256]{1,0:T(8,128)S(1)}, u32[]{:S(2)}, u32[]{:S(2)}) collective-permute-start(f32[256,256]{1,0:T(8,128)S(1)} %bitcast.82), channel_id=1, source_target_pairs={{0,1},{1,0},{2,3},{3,2},{4,5},{5,4},{6,7},{7,6},{8,9},{9,8},{10,11... | collective-permute-start | bytes 786440 | tf_op jit(solution)/shard_map/ppermute | solution.py:23
  111.5 35.7 %all-to-all-start.1 = ((f32[16,32,1024]{2,1,0:T(8,128)}), f32[16,32,1024]{2,1,0:T(8,128)}, u32[]{:S(2)}, u32[]{:S(2)}) async-start(f32[16,32,1024]{2,1,0:T(8,128)} %bitcast.77), calls=%async_computation.1 | async-start | bytes 4194304 | tf_op jit(solution)/shard_map/all_to_all | solution.py:31
  148.9 39.9 %copy-start.2 = (f32[64,1024]{1,0:T(8,128)S(1)}, f32[64,1024]{1,0:T(8,128)}, u32[]{:S(2)}) copy-start(f32[64,1024]{1,0:T(8,128)} %param.10) | copy-start | bytes 786436
  148.9 18.2 %collective-permute-start.12 = (f32[16,1024]{1,0:T(8,128)S(1)}, f32[16,1024]{1,0:T(8,128)S(1)}, u32[]{:S(2)}, u32[]{:S(2)}) collective-permute-start(f32[16,1024]{1,0:T(8,128)S(1)} %get-tuple-element.26), channel_id=1, source_target_pairs={{0,384},{128,256},{256,128},{384,0},{1,385},{129,257},{257,129},{3... | collective-permute-start | bytes 196616 | tf_op jit(solution)/shard_map/ppermute | solution.py:23
  158.0 9.1 %collective-permute-start.10 = (f32[16,1024]{1,0:T(8,128)S(1)}, f32[16,1024]{1,0:T(8,128)S(1)}, u32[]{:S(2)}, u32[]{:S(2)}) collective-permute-start(f32[16,1024]{1,0:T(8,128)S(1)} %get-tuple-element.24), channel_id=1, source_target_pairs={{0,128},{128,0},{256,384},{384,256},{1,129},{129,1},{257,385},{385... | collective-permute-start | bytes 196616 | tf_op jit(solution)/shard_map/ppermute | solution.py:23
  167.2 9.4 %collective-permute-start.13 = (f32[16,1024]{1,0:T(8,128)S(1)}, f32[16,1024]{1,0:T(8,128)S(1)}, u32[]{:S(2)}, u32[]{:S(2)}) collective-permute-start(f32[16,1024]{1,0:T(8,128)S(1)} %add.162), channel_id=1, source_target_pairs={{0,128},{128,0},{256,384},{384,256},{1,129},{129,1},{257,385},{385... | collective-permute-start | bytes 196616 | tf_op jit(solution)/shard_map/ppermute | solution.py:23
  172.4 9.7 %collective-permute-start.11 = (f32[16,1024]{1,0:T(8,128)S(1)}, f32[16,1024]{1,0:T(8,128)S(1)}, u32[]{:S(2)}, u32[]{:S(2)}) collective-permute-start(f32[16,1024]{1,0:T(8,128)S(1)} %add.160), channel_id=1, source_target_pairs={{0,384},{128,256},{256,128},{384,0},{1,385},{129,257},{257,129},{3... | collective-permute-start | bytes 196616 | tf_op jit(solution)/shard_map/ppermute | solution.py:23
  182.2 6.6 %collective-permute-start.14 = (f32[32,1024]{1,0:T(8,128)S(1)}, f32[32,1024]{1,0:T(8,128)S(1)}, u32[]{:S(2)}, u32[]{:S(2)}) collective-permute-start(f32[32,1024]{1,0:T(8,128)S(1)} %get-tuple-element.30), channel_id=1, source_target_pairs={{0,64},{64,0},{1,65},{65,1},{2,66},{66,2},{3,67},{67,3},{4,68},{68... | collective-permute-start | bytes 393224 | tf_op jit(solution)/shard_map/ppermute | solution.py:23
